TPU v7x, 32 devices: a whole 2x2x4 slice. The times are simulated.
32 devices in a mesh: dp: 8 (over z, y), tensor: 4 (over x, core).
Axes of the slice: x: 2, y: 2, z: 4, core: 2. Of those that a mesh axis runs over, the one named last changes fastest.
Arguments:
- tokens: bfloat16 [32768, 768], P(('dp', 'tensor')), may hold values from -6 to 6
- doc_lengths: int32 [32, 16], P('dp'), may hold values from 1 to 512, 1024 in all within a row
- w_query: bfloat16 [768, 768], P('dp', 'tensor'), may hold values from -0.21875 to 0.21875
- w_key: bfloat16 [768, 768], P('dp', 'tensor'), may hold values from -0.21875 to 0.21875
- w_value: bfloat16 [768, 768], P('dp', 'tensor'), may hold values from -0.21875 to 0.21875
- w_out: bfloat16 [768, 768], P('tensor', 'dp'), may hold values from -1.25 to 1.25
- w_up: bfloat16 [768, 3072], P('dp', 'tensor'), may hold values from -0.21875 to 0.21875
- w_down: bfloat16 [3072, 768], P('tensor', 'dp'), may hold values from -0.109375 to 0.109375
- b_query: bfloat16 [12, 64], P('tensor', 'dp'), may hold values from -3 to 3
- b_value: bfloat16 [12, 64], P('tensor', 'dp'), may hold values from -3 to 3
- b_up: bfloat16 [24, 128], P('tensor', 'dp'), may hold values from -3 to 3
- b_out: float32 [768], P(('dp', 'tensor')), may hold values from -3 to 3
- b_down: float32 [768], P(('dp', 'tensor')), may hold values from -3 to 3
- gain_one: float32 [768], P(('dp', 'tensor')), may hold values from 0.1 to 1.9
- shift_one: float32 [768], P(('dp', 'tensor')), may hold values from -3 to 3
- gain_two: float32 [768], P(('dp', 'tensor')), may hold values from 0.1 to 1.9
- shift_two: float32 [768], P(('dp', 'tensor')), may hold values from -3 to 3
- cotangent: bfloat16 [32768, 768], P(('dp', 'tensor')), may hold values from -6 to 6
Outputs:
- layer_out: bfloat16 [32768, 768], P(('dp', 'tensor'))
- grad_tokens: bfloat16 [32768, 768], P(('dp', 'tensor'))
- grad_w_query: float32 [768, 768], P('dp', 'tensor')
- grad_w_key: float32 [768, 768], P('dp', 'tensor')
- grad_w_value: float32 [768, 768], P('dp', 'tensor')
- grad_w_out: float32 [768, 768], P('tensor', 'dp')
- grad_w_up: float32 [768, 3072], P('dp', 'tensor')
- grad_w_down: float32 [3072, 768], P('tensor', 'dp')
- grad_b_query: float32 [12, 64], P('tensor', 'dp')
- grad_b_value: float32 [12, 64], P('tensor', 'dp')
- grad_b_up: float32 [24, 128], P('tensor', 'dp')
- grad_b_out: float32 [768], P(('dp', 'tensor'))
- grad_b_down: float32 [768], P(('dp', 'tensor'))
- grad_gain_one: float32 [768], P(('dp', 'tensor'))
- grad_shift_one: float32 [768], P(('dp', 'tensor'))
- grad_gain_two: float32 [768], P(('dp', 'tensor'))
- grad_shift_two: float32 [768], P(('dp', 'tensor'))
Inputs may be any that keep to these rules, and one draw needn't show every extreme that they name: `doc_lengths`: each row holds the 16 document lengths of one sequence in order and sums to 1024.
All inputs are finite; a program needn't handle non-finite values.
Results may differ from a plain program's by a relative error of at most 0.02.
Values may be sent and summed in bfloat16 or wider, within the bound.
No kernel may reach another device: no remote copies, remote signals or barrier semaphores. Data moves between devices by JAX's collectives and lax.ppermute only.
A program may use at most 192 MiB of HBM per device.

v0:
```python
import jax
import jax.numpy as jnp
from jax import lax
from jax.sharding import PartitionSpec as P

HD = 64
LEN = 1024


epsilon = 1e-06
root_half = 0.7071067811865476
inv_root_tau = 0.3989422804014327
masked_value = -1e30


def normalize(values, norm_gain, norm_shift):
    average = jnp.mean(values, axis=-1, keepdims=True)
    centred = values - average
    variance = jnp.mean(centred * centred, axis=-1, keepdims=True)
    inv_scale = lax.rsqrt(variance + epsilon)
    unit_rows = centred * inv_scale
    return (unit_rows * norm_gain + norm_shift, unit_rows, inv_scale)


def normalize_back(grad_out, unit_rows, inv_scale, norm_gain):
    grad_unit = grad_out * norm_gain
    middle = grad_unit - jnp.mean(grad_unit, axis=-1, keepdims=True)
    middle = middle - unit_rows * jnp.mean(grad_unit * unit_rows, axis=-1, keepdims=True)
    return inv_scale * middle


def gelu_parts(up_pre):
    normal_cdf = 0.5 * (1.0 + lax.erf(up_pre * root_half))
    return (
        up_pre * normal_cdf,
        normal_cdf + up_pre * inv_root_tau * jnp.exp(-0.5 * up_pre * up_pre),
    )


def segment_ids(doc_lengths, length):
    bounds = jnp.cumsum(doc_lengths, axis=-1)
    places = lax.broadcasted_iota(jnp.int32, (1, length, 1), 1)
    return jnp.sum((bounds[:, None, :] <= places).astype(jnp.int32), axis=-1)


def block_scores(query_block, key_seq, seg_block, seg_seq):
    scale = query_block.shape[-1] ** (-0.5)
    scores = (
        jnp.einsum("qhd,khd->hqk", query_block, key_seq, preferred_element_type=jnp.float32) * scale
    )
    allowed = seg_block[:, None] == seg_seq[None, :]
    return jnp.where(allowed[None], scores, masked_value)


def attention_forward(queries, keys_all, values_all, segments):
    seq_count, length = segments.shape
    head_count = queries.shape[1] // HD
    block_rows = min(512, length)
    shaped = (seq_count, length, head_count, HD)

    def one_sequence(inputs):
        query_one, key_one, value_one, seg_one = inputs
        outputs = []
        totals = []
        for offset in range(0, length, block_rows):
            ending = offset + block_rows
            scores = block_scores(
                query_one[offset:ending], key_one, seg_one[offset:ending], seg_one
            )
            row_top = jnp.max(scores, axis=-1, keepdims=True)
            weights = jnp.exp(scores - row_top)
            row_total = jnp.sum(weights, axis=-1, keepdims=True)
            probability = (weights / row_total).astype(jnp.bfloat16)
            mixture = jnp.einsum(
                "hqk,khd->qhd", probability, value_one, preferred_element_type=jnp.float32
            )
            outputs.append(mixture.astype(jnp.bfloat16))
            totals.append(row_top[..., 0] + jnp.log(row_total[..., 0]))
        return (jnp.concatenate(outputs, axis=0), jnp.concatenate(totals, axis=1))

    mixture, log_totals = lax.map(
        one_sequence,
        (queries.reshape(shaped), keys_all.reshape(shaped), values_all.reshape(shaped), segments),
    )
    return (mixture.reshape(seq_count * length, head_count * HD), log_totals)


def attention_backward(queries, keys_all, values_all, segments, log_totals, grad_mixture):
    seq_count, length = segments.shape
    head_count = queries.shape[1] // HD
    block_rows = min(512, length)
    shaped = (seq_count, length, head_count, HD)
    scale = HD ** (-0.5)

    def one_sequence(inputs):
        query_one, key_one, value_one, seg_one, grad_one, total_one = inputs
        grad_keys = jnp.zeros(key_one.shape, jnp.float32)
        grad_values = jnp.zeros(value_one.shape, jnp.float32)
        grad_queries = []
        for offset in range(0, length, block_rows):
            ending = offset + block_rows
            scores = block_scores(
                query_one[offset:ending], key_one, seg_one[offset:ending], seg_one
            )
            probability = jnp.exp(scores - total_one[:, offset:ending, None])
            grad_block = grad_one[offset:ending]
            grad_prob = jnp.einsum(
                "qhd,khd->hqk", grad_block, value_one, preferred_element_type=jnp.float32
            )
            inner = jnp.sum(probability * grad_prob, axis=-1, keepdims=True)
            grad_scores = (probability * (grad_prob - inner)).astype(jnp.bfloat16)
            block_query = jnp.einsum(
                "hqk,khd->qhd", grad_scores, key_one, preferred_element_type=jnp.float32
            )
            grad_queries.append((block_query * scale).astype(jnp.bfloat16))
            grad_keys = (
                grad_keys
                + jnp.einsum(
                    "hqk,qhd->khd",
                    grad_scores,
                    query_one[offset:ending],
                    preferred_element_type=jnp.float32,
                )
                * scale
            )
            grad_values = grad_values + jnp.einsum(
                "hqk,qhd->khd",
                probability.astype(jnp.bfloat16),
                grad_block,
                preferred_element_type=jnp.float32,
            )
        return (
            jnp.concatenate(grad_queries, axis=0),
            grad_keys.astype(jnp.bfloat16),
            grad_values.astype(jnp.bfloat16),
        )

    grad_q, grad_k, grad_v = lax.map(
        one_sequence,
        (
            queries.reshape(shaped),
            keys_all.reshape(shaped),
            values_all.reshape(shaped),
            segments,
            grad_mixture.reshape(shaped),
            log_totals,
        ),
    )
    flat = (seq_count * length, head_count * HD)
    return (grad_q.reshape(flat), grad_k.reshape(flat), grad_v.reshape(flat))


def per_device(
    tokens,
    doc_lengths,
    w_query,
    w_key,
    w_value,
    w_out,
    w_up,
    w_down,
    b_query,
    b_value,
    b_up,
    b_out,
    b_down,
    gain_one,
    shift_one,
    gain_two,
    shift_two,
    cotangent,
):
    segments = segment_ids(doc_lengths, LEN)
    gathered = (
        lax.all_gather(w_query, "dp", axis=0, tiled=True),
        lax.all_gather(w_key, "dp", axis=0, tiled=True),
        lax.all_gather(w_value, "dp", axis=0, tiled=True),
        lax.all_gather(w_out, "dp", axis=1, tiled=True),
        lax.all_gather(w_up, "dp", axis=0, tiled=True),
        lax.all_gather(w_down, "dp", axis=1, tiled=True),
        lax.all_gather(b_query, "dp", axis=1, tiled=True),
        lax.all_gather(b_value, "dp", axis=1, tiled=True),
        lax.all_gather(b_up, "dp", axis=1, tiled=True),
    )
    (
        full_query,
        full_key,
        full_value,
        full_out,
        full_up,
        full_down,
        bias_query,
        bias_value,
        bias_up,
    ) = gathered
    vectors = (
        lax.all_gather(b_out, ("dp", "tensor"), axis=0, tiled=True),
        lax.all_gather(b_down, ("dp", "tensor"), axis=0, tiled=True),
        lax.all_gather(gain_one, ("dp", "tensor"), axis=0, tiled=True),
        lax.all_gather(shift_one, ("dp", "tensor"), axis=0, tiled=True),
        lax.all_gather(gain_two, ("dp", "tensor"), axis=0, tiled=True),
        lax.all_gather(shift_two, ("dp", "tensor"), axis=0, tiled=True),
    )
    bias_out, bias_down, norm_gain_one, norm_shift_one, norm_gain_two, norm_shift_two = vectors
    local_rows = tokens.shape[0]
    tokens_all = lax.all_gather(tokens, "tensor", axis=0, tiled=True)
    queries = (
        jnp.dot(tokens_all, full_query, preferred_element_type=jnp.float32)
        + bias_query.reshape(-1).astype(jnp.float32)
    ).astype(jnp.bfloat16)
    keys_all = jnp.dot(tokens_all, full_key, preferred_element_type=jnp.float32).astype(
        jnp.bfloat16
    )
    values_all = (
        jnp.dot(tokens_all, full_value, preferred_element_type=jnp.float32)
        + bias_value.reshape(-1).astype(jnp.float32)
    ).astype(jnp.bfloat16)
    mixture, log_totals = attention_forward(queries, keys_all, values_all, segments)
    piece = lax.slice_in_dim(mixture, 0, local_rows * lax.axis_size("tensor"), axis=0)
    attn_part = lax.psum_scatter(
        jnp.dot(piece, full_out, preferred_element_type=jnp.float32).astype(jnp.bfloat16),
        "tensor",
        scatter_dimension=0,
        tiled=True,
    ).astype(jnp.float32)
    residual_one = attn_part + bias_out + tokens.astype(jnp.float32)
    first, unit_one, scale_one = normalize(residual_one, norm_gain_one, norm_shift_one)
    first_all = lax.all_gather(first.astype(jnp.bfloat16), "tensor", axis=0, tiled=True)
    up_pre = jnp.dot(first_all, full_up, preferred_element_type=jnp.float32) + bias_up.reshape(
        -1
    ).astype(jnp.float32)
    activated, slope = gelu_parts(up_pre)
    activated = activated.astype(jnp.bfloat16)
    piece = lax.slice_in_dim(activated, 0, local_rows * lax.axis_size("tensor"), axis=0)
    ffn_part = lax.psum_scatter(
        jnp.dot(piece, full_down, preferred_element_type=jnp.float32).astype(jnp.bfloat16),
        "tensor",
        scatter_dimension=0,
        tiled=True,
    ).astype(jnp.float32)
    residual_two = ffn_part + bias_down + first
    result, unit_two, scale_two = normalize(residual_two, norm_gain_two, norm_shift_two)
    grad_out = cotangent.astype(jnp.float32)
    grad_two = normalize_back(grad_out, unit_two, scale_two, norm_gain_two)
    grad_gain_two = jnp.sum(grad_out * unit_two, axis=0)
    grad_shift_two = jnp.sum(grad_out, axis=0)
    grad_bias_down = jnp.sum(grad_two, axis=0)
    grad_two_all = lax.all_gather(grad_two.astype(jnp.bfloat16), "tensor", axis=0, tiled=True)
    grad_w_down = jnp.einsum(
        "tf,td->fd", activated, grad_two_all, preferred_element_type=jnp.float32
    )
    grad_active = jnp.einsum(
        "td,fd->tf", grad_two_all, full_down, preferred_element_type=jnp.float32
    )
    grad_up = (grad_active * slope).astype(jnp.bfloat16)
    grad_bias_up = jnp.sum(grad_up, axis=0, dtype=jnp.float32)
    grad_w_up = jnp.einsum("td,tf->df", first_all, grad_up, preferred_element_type=jnp.float32)
    piece = lax.slice_in_dim(grad_up, 0, local_rows * lax.axis_size("tensor"), axis=0)
    grad_first = (
        lax.psum_scatter(
            jnp.einsum("tf,df->td", piece, full_up, preferred_element_type=jnp.float32).astype(
                jnp.bfloat16
            ),
            "tensor",
            scatter_dimension=0,
            tiled=True,
        ).astype(jnp.float32)
        + grad_two
    )
    grad_one = normalize_back(grad_first, unit_one, scale_one, norm_gain_one)
    grad_gain_one = jnp.sum(grad_first * unit_one, axis=0)
    grad_shift_one = jnp.sum(grad_first, axis=0)
    grad_bias_out = jnp.sum(grad_one, axis=0)
    grad_one_all = lax.all_gather(grad_one.astype(jnp.bfloat16), "tensor", axis=0, tiled=True)
    grad_w_out = jnp.einsum("th,td->hd", mixture, grad_one_all, preferred_element_type=jnp.float32)
    grad_mixture = jnp.einsum(
        "td,hd->th", grad_one_all, full_out, preferred_element_type=jnp.float32
    ).astype(jnp.bfloat16)
    grad_queries, grad_keys, grad_values = attention_backward(
        queries, keys_all, values_all, segments, log_totals, grad_mixture
    )
    grad_bias_query = jnp.sum(grad_queries, axis=0, dtype=jnp.float32)
    grad_bias_value = jnp.sum(grad_values, axis=0, dtype=jnp.float32)
    grad_w_query = jnp.einsum(
        "td,th->dh", tokens_all, grad_queries, preferred_element_type=jnp.float32
    )
    grad_w_key = jnp.einsum("td,th->dh", tokens_all, grad_keys, preferred_element_type=jnp.float32)
    grad_w_value = jnp.einsum(
        "td,th->dh", tokens_all, grad_values, preferred_element_type=jnp.float32
    )
    part_query = lax.slice_in_dim(grad_queries, 0, local_rows * lax.axis_size("tensor"), axis=0)
    part_key = lax.slice_in_dim(grad_keys, 0, local_rows * lax.axis_size("tensor"), axis=0)
    part_value = lax.slice_in_dim(grad_values, 0, local_rows * lax.axis_size("tensor"), axis=0)
    summed = jnp.einsum("th,dh->td", part_query, full_query, preferred_element_type=jnp.float32)
    summed = summed + jnp.einsum(
        "th,dh->td", part_key, full_key, preferred_element_type=jnp.float32
    )
    grad_input = (
        lax.psum_scatter(
            (
                summed
                + jnp.einsum(
                    "th,dh->td", part_value, full_value, preferred_element_type=jnp.float32
                )
            ).astype(jnp.bfloat16),
            "tensor",
            scatter_dimension=0,
            tiled=True,
        ).astype(jnp.float32)
        + grad_one
    )
    sent = (
        lax.psum_scatter(grad_w_query, "dp", scatter_dimension=0, tiled=True),
        lax.psum_scatter(grad_w_key, "dp", scatter_dimension=0, tiled=True),
        lax.psum_scatter(grad_w_value, "dp", scatter_dimension=0, tiled=True),
        lax.psum_scatter(grad_w_out, "dp", scatter_dimension=1, tiled=True),
        lax.psum_scatter(grad_w_up, "dp", scatter_dimension=0, tiled=True),
        lax.psum_scatter(grad_w_down, "dp", scatter_dimension=1, tiled=True),
        lax.psum_scatter(grad_bias_query.reshape(-1, HD), "dp", scatter_dimension=1, tiled=True),
        lax.psum_scatter(grad_bias_value.reshape(-1, HD), "dp", scatter_dimension=1, tiled=True),
        lax.psum_scatter(grad_bias_up.reshape(-1, 128), "dp", scatter_dimension=1, tiled=True),
    )
    vector_sums = (
        lax.psum_scatter(grad_bias_out, ("dp", "tensor"), scatter_dimension=0, tiled=True),
        lax.psum_scatter(grad_bias_down, ("dp", "tensor"), scatter_dimension=0, tiled=True),
        lax.psum_scatter(grad_gain_one, ("dp", "tensor"), scatter_dimension=0, tiled=True),
        lax.psum_scatter(grad_shift_one, ("dp", "tensor"), scatter_dimension=0, tiled=True),
        lax.psum_scatter(grad_gain_two, ("dp", "tensor"), scatter_dimension=0, tiled=True),
        lax.psum_scatter(grad_shift_two, ("dp", "tensor"), scatter_dimension=0, tiled=True),
    )
    return (
        result.astype(jnp.bfloat16),
        grad_input.astype(jnp.bfloat16),
        sent[0],
        sent[1],
        sent[2],
        sent[3],
        sent[4],
        sent[5],
        sent[6],
        sent[7],
        sent[8],
        vector_sums[0],
        vector_sums[1],
        vector_sums[2],
        vector_sums[3],
        vector_sums[4],
        vector_sums[5],
    )


def solution(mesh):
    placed = (
        P(("dp", "tensor"), None),
        P("dp", None),
        P("dp", "tensor"),
        P("dp", "tensor"),
        P("dp", "tensor"),
        P("tensor", "dp"),
        P("dp", "tensor"),
        P("tensor", "dp"),
        P("tensor", "dp"),
        P("tensor", "dp"),
        P("tensor", "dp"),
        P(("dp", "tensor")),
        P(("dp", "tensor")),
        P(("dp", "tensor")),
        P(("dp", "tensor")),
        P(("dp", "tensor")),
        P(("dp", "tensor")),
        P(("dp", "tensor"), None),
    )
    return jax.shard_map(
        per_device,
        mesh=mesh,
        in_specs=placed,
        out_specs=(
            P(("dp", "tensor"), None),
            P(("dp", "tensor"), None),
            P("dp", "tensor"),
            P("dp", "tensor"),
            P("dp", "tensor"),
            P("tensor", "dp"),
            P("dp", "tensor"),
            P("tensor", "dp"),
            P("tensor", "dp"),
            P("tensor", "dp"),
            P("tensor", "dp"),
            P(("dp", "tensor")),
            P(("dp", "tensor")),
            P(("dp", "tensor")),
            P(("dp", "tensor")),
            P(("dp", "tensor")),
            P(("dp", "tensor")),
        ),
        check_vma=False,
    )
```

profile of v0, /device:TPU:0, one launch (start us, length us, event | category | flops | bytes accessed | tf_op | source)
XLA Modules:
  0.0 1349.2 jit_solution(8543374420555080612)
XLA Ops:
  9.7 22.5 %all-gather.1 = bf16[8,8,3]{1,2,0:T(4,128)(2,1)S(1)} all-gather(bf16[1,8,3]{1,2,0:T(4,128)(2,1)} %bitcast.319), channel_id=1, replica_groups=mesh['dp'=8,'tensor'=4] {'dp'}, dimensions={0}, use_global_device_ids=true | all-gather | bytes 432 | tf_op jit(solution)/shard_map/all_gather | solution.py:181
  32.9 16.6 %all-gather = bf16[8,8,3]{1,2,0:T(4,128)(2,1)S(1)} all-gather(bf16[1,8,3]{1,2,0:T(4,128)(2,1)} %bitcast.320), channel_id=1, replica_groups=mesh['dp'=8,'tensor'=4] {'dp'}, dimensions={0}, use_global_device_ids=true | all-gather | bytes 432 | tf_op jit(solution)/shard_map/all_gather | solution.py:182
  50.7 31.2 %all_gather.63 = bf16[192,768]{0,1:T(8,128)(2,1)S(1)} all-gather(bf16[192,96]{0,1:T(8,128)(2,1)S(1)} %copy.104), channel_id=1, replica_groups=mesh['dp'=8,'tensor'=4] {'dp'}, dimensions={1}, use_global_device_ids=true | all-gather | bytes 331776 | tf_op jit(solution)/shard_map/all_gather | solution.py:178
  81.9 33.3 %all_gather.60 = bf16[768,192]{1,0:T(8,128)(2,1)} all-gather(bf16[96,192]{1,0:T(8,128)(2,1)} %param.24), channel_id=1, replica_groups=mesh['dp'=8,'tensor'=4] {'dp'}, dimensions={0}, use_global_device_ids=true | all-gather | bytes 331776 | tf_op jit(solution)/shard_map/all_gather | solution.py:175
  115.2 33.3 %all_gather.62 = bf16[768,192]{1,0:T(8,128)(2,1)} all-gather(bf16[96,192]{1,0:T(8,128)(2,1)} %param.25), channel_id=1, replica_groups=mesh['dp'=8,'tensor'=4] {'dp'}, dimensions={0}, use_global_device_ids=true | all-gather | bytes 331776 | tf_op jit(solution)/shard_map/all_gather | solution.py:176
  148.6 31.0 %all_gather.58 = bf16[768,192]{1,0:T(8,128)(2,1)S(1)} all-gather(bf16[96,192]{1,0:T(8,128)(2,1)S(1)} %copy-done.38), channel_id=1, replica_groups=mesh['dp'=8,'tensor'=4] {'dp'}, dimensions={0}, use_global_device_ids=true | all-gather | bytes 331776 | tf_op jit(solution)/shard_map/all_gather | solution.py:177
  180.3 5.0 fusion.95
  188.1 5.0 fusion.96
  195.3 5.0 convolution_convert_fusion.4
  205.9 52.2 %while.26 = (s32[]{:T(128)}, bf16[4,1024,3,64]{1,3,2,0:T(8,128)(2,1)}, f32[4,3,1024]{2,1,0:T(4,128)}, bf16[4,1024,3,64]{1,3,2,0:T(8,128)(2,1)}, s32[4,1024]{1,0:...) while((s32[]{:T(128)}, ...), condition=%wide.region_7.8_spmd, body=%wide.region_2.7_spmd.sunk | while | flops 845086720 | bytes 51542704 | solution.py:81
  209.6 3.5 fusion.189
  222.6 3.5 fusion.189
  235.6 3.5 fusion.189
  248.6 3.5 fusion.189
  258.1 3.2 copy.103
  263.1 4.5 convolution_convert_fusion
  278.1 39.3 %all-reduce.15 = (f32[768]{0:T(1024)}, f32[768]{0:T(1024)}, f32[768]{0:T(1024)}, f32[768]{0:T(1024)}, f32[768]{0:T(1024)}) all-reduce(f32[768]{0:T(1024)} %dynamic-update-slice.2, f32[768]{0:T(1024)} %dynamic-update-slice.1, f32[768]{0:T(1024)} %dynamic-update-slice, ...), channel_id=1, replica_groups=mesh['dp'=8,'tensor'=4] {'dp','tensor'}, use_global_device_ids=true, to_apply=%add.2 | all-reduce | flops 3840 | bytes 30720
  317.4 8.2 reduce-scatter.24.cloned.1.call-done
  331.9 26.1 %all-gather.2 = bf16[8,16,6]{1,2,0:T(8,128)(2,1)S(1)} all-gather(bf16[1,16,6]{1,2,0:T(8,128)(2,1)} %bitcast.318), channel_id=1, replica_groups=mesh['dp'=8,'tensor'=4] {'dp'}, dimensions={0}, use_global_device_ids=true | all-gather | bytes 1728 | tf_op jit(solution)/shard_map/all_gather | solution.py:183
  360.0 17.5 %all-gather.12.cloned.1.call-done = bf16[4096,768]{1,0:T(8,128)(2,1)} async-done(((bf16[1024,768]{1,0:T(8,128)(2,1)}), bf16[4096,768]{1,0:T(8,128)(2,1)}) %all-gather.12.cloned.1.call-update) | async-done | bytes 6291472 | tf_op jit(solution)/shard_map/all_gather | solution.py:228
  377.5 12.1 multiply_convert_fusion.2
  389.6 31.7 %all-gather.16.cloned.1.call-done = bf16[768,768]{0,1:T(8,128)(2,1)} async-done(((bf16[768,96]{0,1:T(8,128)(2,1)}), bf16[768,768]{0,1:T(8,128)(2,1)}) %all-gather.16.cloned.1.call-update) | async-done | bytes 1179664 | tf_op jit(solution)/shard_map/all_gather | solution.py:180
  421.4 9.2 convolution_convert_fusion.2
  430.6 56.8 %reduce-scatter.26.cloned.1.call-done = bf16[1024,768]{1,0:T(8,128)(2,1)} async-done(((bf16[4096,768]{1,0:T(8,128)(2,1)}), bf16[1024,768]{1,0:T(8,128)(2,1)}) %reduce-scatter.26.cloned.1.call-update) | async-done | bytes 1572880 | tf_op jit(solution)/shard_map/reduce_scatter | solution.py:235
  498.2 46.5 %all-gather.18.cloned.1.call-done = bf16[4096,768]{1,0:T(8,128)(2,1)} async-done(((bf16[1024,768]{1,0:T(8,128)(2,1)}), bf16[4096,768]{1,0:T(8,128)(2,1)}) %all-gather.18.cloned.1.call-update) | async-done | bytes 6291472 | tf_op jit(solution)/shard_map/all_gather | solution.py:248
  544.7 13.1 convert_reduce_fusion
  560.4 7.1 convolution_convert_fusion.1
  567.6 58.3 %reduce-scatter.28.cloned.1.call-done = bf16[1024,768]{1,0:T(8,128)(2,1)} async-done(((bf16[4096,768]{1,0:T(8,128)(2,1)}), bf16[1024,768]{1,0:T(8,128)(2,1)}) %reduce-scatter.28.cloned.1.call-update) | async-done | bytes 1572880 | tf_op jit(solution)/shard_map/reduce_scatter | solution.py:260
  625.9 5.3 multiply_reduce_fusion.2
  635.9 45.0 %all-gather.20.cloned.1.call-done = bf16[4096,768]{1,0:T(8,128)(2,1)} async-done(((bf16[1024,768]{1,0:T(8,128)(2,1)}), bf16[4096,768]{1,0:T(8,128)(2,1)}) %all-gather.20.cloned.1.call-update) | async-done | bytes 6291472 | tf_op jit(solution)/shard_map/all_gather | solution.py:274
  680.9 5.0 convolution_convert_fusion.3
  694.2 154.3 %while.27 = (s32[]{:T(128)}, bf16[4,1024,3,64]{1,3,2,0:T(8,128)(2,1)}, bf16[4,1024,3,64]{1,3,2,0:T(8,128)(2,1)}, bf16[4,1024,3,64]{1,3,2,0:T(8,128)(2,1)S(1)}, b...) while((s32[]{:T(128)}, ...), condition=%wide.region_22.23_spmd, body=%wide.region_19.22_spmd.sunk | while | flops 2063660032 | bytes 151801680 | solution.py:138
  703.7 5.7 multiply_reduce_fusion.9
  709.4 5.3 multiply_reduce_fusion.10
  714.7 7.6 multiply_convert_fusion.4
  722.3 3.1 fusion.207
  742.2 5.7 multiply_reduce_fusion.9
  747.9 5.3 multiply_reduce_fusion.10
  753.2 7.6 multiply_convert_fusion.4
  760.8 3.1 fusion.207
  780.6 5.7 multiply_reduce_fusion.9
  786.3 5.3 multiply_reduce_fusion.10
  791.6 7.6 multiply_convert_fusion.4
  819.0 5.7 multiply_reduce_fusion.9
  824.7 5.3 multiply_reduce_fusion.10
  830.0 7.6 multiply_convert_fusion.4
  854.9 6.4 fusion.113
  861.4 3.6 convolution_bitcast_fusion
  865.0 7.8 fusion.112
  876.0 13.2 add_convert_fusion
  889.2 10.1 fusion.114
  899.4 10.1 fusion.115
  909.7 5.5 convolution_bitcast_fusion.3
  917.5 5.5 convolution_bitcast_fusion.2
  928.2 5.5 convolution_bitcast_fusion.1
  936.5 21.5 %all-reduce.16 = (f32[3,64]{1,0:T(4,128)S(1)}, f32[3,64]{1,0:T(4,128)S(1)}) all-reduce(f32[3,64]{1,0:T(4,128)S(1)} %convert_reduce_fusion.3, f32[3,64]{1,0:T(4,128)S(1)} %convert_reduce_fusion.2), channel_id=12, replica_groups=mesh['dp'=8,'tensor'=4] {'dp'}, use_global_device_ids=true, to_apply=%region_31.32.clone | all-reduce | flops 384 | bytes 3072
  961.0 37.1 %reduce-scatter.30.cloned.1.call-done = bf16[1024,768]{1,0:T(8,128)(2,1)} async-done(((bf16[4096,768]{1,0:T(8,128)(2,1)}), bf16[1024,768]{1,0:T(8,128)(2,1)}) %reduce-scatter.30.cloned.1.call-update) | async-done | bytes 1572880 | tf_op jit(solution)/shard_map/reduce_scatter | solution.py:299
  998.1 4.1 add_convert_fusion.1
  1002.2 40.5 %all-reduce.14 = (f32[768]{0:T(1024)S(1)}, f32[768]{0:T(1024)S(1)}, f32[768]{0:T(1024)S(1)}, f32[768]{0:T(1024)S(1)}, f32[768]{0:T(1024)S(1)}, /*index=5*/f32[768]{0:T(1024)S(1)}, f32[768]{0:T(1024)S(1)}) all-reduce(f32[768]{0:T(1024)S(1)} %dynamic-update-slice.5, ...), channel_id=1, replica_groups=mesh['dp'=8,'tensor'=4] {'dp','tensor'}, use_global_device_ids=true, to_apply=%add.5 | all-reduce | flops 5376 | bytes 43008
  1047.9 24.0 %reduce-scatter.32.cloned.1.call-done = f32[96,768]{1,0:T(8,128)} async-done(((f32[768,768]{1,0:T(8,128)}), f32[96,768]{1,0:T(8,128)}) %reduce-scatter.32.cloned.1.call-update) | async-done | bytes 294928 | tf_op jit(solution)/shard_map/reduce_scatter | solution.py:317
  1071.9 72.7 %reduce-scatter.34.cloned.1.call-done = f32[768,96]{0,1:T(8,128)} async-done(((f32[768,768]{0,1:T(8,128)}), f32[768,96]{0,1:T(8,128)}) %reduce-scatter.34.cloned.1.call-update) | async-done | bytes 294928 | tf_op jit(solution)/shard_map/reduce_scatter | solution.py:318
  1144.6 65.8 %reduce-scatter.36.cloned.1.call-done = f32[96,192]{1,0:T(8,128)} async-done(((f32[768,192]{1,0:T(8,128)}), f32[96,192]{1,0:T(8,128)}) %reduce-scatter.36.cloned.1.call-update) | async-done | bytes 73744
  1210.4 65.5 %reduce-scatter.38.cloned.1.call-done = f32[96,192]{1,0:T(8,128)} async-done(((f32[768,192]{1,0:T(8,128)}), f32[96,192]{1,0:T(8,128)}) %reduce-scatter.38.cloned.1.call-update) | async-done | bytes 73744
  1275.8 65.7 %reduce-scatter.40.cloned.1.call-done = f32[96,192]{1,0:T(8,128)} async-done(((f32[768,192]{1,0:T(8,128)}), f32[96,192]{1,0:T(8,128)}) %reduce-scatter.40.cloned.1.call-update) | async-done | bytes 73744
  (363 shorter events, 200.0 us)
Async XLA Ops:
  8.0 140.5 %copy-start.38 = (bf16[96,192]{1,0:T(8,128)(2,1)S(1)}, bf16[96,192]{1,0:T(8,128)(2,1)}, u32[]{:S(2)}) copy-start(bf16[96,192]{1,0:T(8,128)(2,1)} %param.26) | copy-start | bytes 110596
  8.0 171.5 %all-gather.10.cloned.1.call-start = ((), (), s32[]{:S(2)}) async-start(), calls=%async_computation.11 | async-start | bytes 7864320 | tf_op jit(solution)/shard_map/all_gather | solution.py:206
  8.8 316.8 %reduce-scatter.24.cloned.1.call-start = ((), (), s32[]{:S(2)}) async-start(), calls=%async_computation.12 | async-start | bytes 7864320 | tf_op jit(solution)/shard_map/reduce_scatter | solution.py:220
  209.6 3.5 copy-start.10
  222.6 3.5 copy-start.10
  235.6 3.5 copy-start.10
  248.6 3.5 copy-start.10
  258.1 3.8 copy-start.8
  267.6 57.9 %copy-start.5 = (bf16[1024,768]{1,0:T(8,128)(2,1)S(1)}, bf16[1024,768]{1,0:T(8,128)(2,1)}, u32[]{:S(2)}) copy-start(bf16[1024,768]{1,0:T(8,128)(2,1)} %param.22) | copy-start | bytes 4718596
  267.7 92.4 %all-gather.14.cloned.1.call-start = ((), (), s32[]{:S(2)}) async-start(), calls=%async_computation.14 | async-start | bytes 1327104 | tf_op jit(solution)/shard_map/all_gather | solution.py:179
  268.2 109.3 %all-gather.12.cloned.1.call-start = ((), (), s32[]{:S(2)}) async-start(), calls=%async_computation.13 | async-start | bytes 7864320 | tf_op jit(solution)/shard_map/all_gather | solution.py:228
  325.6 3.6 copy-start.34
  325.6 3.6 copy-start.44
  331.3 90.1 %all-gather.16.cloned.1.call-start = ((), (), s32[]{:S(2)}) async-start(), calls=%async_computation.15 | async-start | bytes 1327104 | tf_op jit(solution)/shard_map/all_gather | solution.py:180
  331.8 155.6 %reduce-scatter.26.cloned.1.call-start = ((), (), s32[]{:S(2)}) async-start(), calls=%async_computation.16 | async-start | bytes 7864320 | tf_op jit(solution)/shard_map/reduce_scatter | solution.py:235
  430.6 114.1 %all-gather.18.cloned.1.call-start = ((), (), s32[]{:S(2)}) async-start(), calls=%async_computation.17 | async-start | bytes 7864320 | tf_op jit(solution)/shard_map/all_gather | solution.py:248
  490.5 4.9 copy-start.3
  490.5 4.8 copy-start.32
  491.0 7.1 copy-start.36
  498.1 127.7 %reduce-scatter.28.cloned.1.call-start = ((), (), s32[]{:S(2)}) async-start(), calls=%async_computation.18 | async-start | bytes 7864320 | tf_op jit(solution)/shard_map/reduce_scatter | solution.py:260
  544.7 15.7 %copy-start.48 = (bf16[768,768]{1,0:T(8,128)(2,1)S(1)}, bf16[768,768]{1,0:T(8,128)(2,1)}, u32[]{:S(2)}) copy-start(bf16[768,768]{1,0:T(8,128)(2,1)} %all-gather.14.cloned.1.call-done) | copy-start | bytes 3538948
  567.5 113.4 %all-gather.20.cloned.1.call-start = ((), (), s32[]{:S(2)}) async-start(), calls=%async_computation.19 | async-start | bytes 7864320 | tf_op jit(solution)/shard_map/all_gather | solution.py:274
  625.9 5.3 copy-start.7
  625.9 5.3 copy-start.9
  625.9 5.3 copy-start.18
  625.9 5.4 copy-start.27
  625.9 5.4 copy-start.29
  625.9 5.4 copy-start.31
  625.9 5.4 copy-start.35
  634.4 292.5 %reduce-scatter.44.cloned.1.call-start = ((), (), s32[]{:S(2)}) async-start(), calls=%async_computation.27 | async-start | bytes 73728
  635.9 323.5 %reduce-scatter.42.cloned.1.call-start = ((), (), s32[]{:S(2)}) async-start(), calls=%async_computation.26 | async-start | bytes 884736
  694.4 7.4 copy-start.1
  703.7 5.7 copy-start.11
  729.5 3.3 copy-start.2
  729.5 3.3 copy-start.12
  732.8 7.4 copy-start.1
  742.2 5.7 copy-start.11
  771.3 7.4 copy-start.1
  780.6 5.7 copy-start.11
  806.4 3.3 copy-start.12
  809.7 7.4 copy-start.1
  819.0 5.7 copy-start.11
  848.5 3.4 copy-start.13
  853.1 8.2 slice-start
  854.9 6.4 slice-start.1
  854.9 6.4 copy-start.15
  861.4 3.6 copy-start.25
  875.7 122.4 %reduce-scatter.30.cloned.1.call-start = ((), (), s32[]{:S(2)}) async-start(), calls=%async_computation.20 | async-start | bytes 7864320 | tf_op jit(solution)/shard_map/reduce_scatter | solution.py:299
  889.2 182.7 %reduce-scatter.32.cloned.1.call-start = ((), (), s32[]{:S(2)}) async-start(), calls=%async_computation.21 | async-start | bytes 2654208 | tf_op jit(solution)/shard_map/reduce_scatter | solution.py:317
  899.4 245.2 %reduce-scatter.34.cloned.1.call-start = ((), (), s32[]{:S(2)}) async-start(), calls=%async_computation.22 | async-start | bytes 2654208 | tf_op jit(solution)/shard_map/reduce_scatter | solution.py:318
  909.6 300.7 %reduce-scatter.36.cloned.1.call-start = ((), (), s32[]{:S(2)}) async-start(), calls=%async_computation.23 | async-start | bytes 884736
  917.4 7.9 copy-start.50
  917.4 9.1 copy-start.49
  917.4 358.4 %reduce-scatter.38.cloned.1.call-start = ((), (), s32[]{:S(2)}) async-start(), calls=%async_computation.24 | async-start | bytes 884736
  925.3 416.3 %reduce-scatter.40.cloned.1.call-start = ((), (), s32[]{:S(2)}) async-start(), calls=%async_computation.25 | async-start | bytes 884736
  998.1 4.1 copy-start.41
  998.1 4.1 copy-start.42
  998.1 4.1 copy-start.43
  998.1 4.1 copy-start.45
  998.1 4.1 copy-start.46
  998.1 48.1 %copy-start.4 = (f32[1024,768]{1,0:T(8,128)S(1)}, f32[1024,768]{1,0:T(8,128)}, u32[]{:S(2)}) copy-start(f32[1024,768]{1,0:T(8,128)} %copy-done.3) | copy-start | bytes 9437188
  998.1 48.1 %copy-start.33 = (f32[1024]{0:T(1024)S(1)}, f32[1024]{0:T(1024)}, u32[]{:S(2)}) copy-start(f32[1024]{0:T(1024)} %copy-done.32) | copy-start | bytes 12292
  998.1 48.1 %copy-start.37 = (f32[1024]{0:T(1024)S(1)}, f32[1024]{0:T(1024)}, u32[]{:S(2)}) copy-start(f32[1024]{0:T(1024)} %copy-done.36) | copy-start | bytes 12292
  998.1 48.1 %copy-start.40 = (f32[768]{0:T(1024)S(1)}, f32[768]{0:T(1024)}, u32[]{:S(2)}) copy-start(f32[768]{0:T(1024)} %get-tuple-element.338) | copy-start | bytes 9220
  (28 other events, 61.8 us)
Sparse Core Ops, SparseCore 0:
  10.4 49.0 all-gather.9
  267.8 57.7 reduce-scatter.23
  498.3 46.3 all-gather.17
  634.5 46.3 all-gather.19
Sparse Core Ops, SparseCore 1:
  270.6 39.8 all-gather.13
  331.3 46.1 all-gather.11
  379.8 41.5 all-gather.15
  430.7 56.7 reduce-scatter.25
  567.6 58.2 reduce-scatter.27
  639.5 61.4 reduce-scatter.43
  875.8 62.5 reduce-scatter.41
  940.8 57.2 reduce-scatter.29
  1002.4 69.4 reduce-scatter.31
  1076.4 68.1 reduce-scatter.33
  1148.7 61.6 reduce-scatter.35
  1214.2 61.5 reduce-scatter.37
  1279.9 61.6 reduce-scatter.39
where the time goes:
time: 1360 us; the launch traced here: 1350 us
  waiting for transfers between devices  597 us (44%)
  blocking collectives  295 us (22%)
  matrix products  276 us (20%)
  other arithmetic  88.6 us (7%)
  local copies, waits for them, and re-layouts  73.7 us (5%)
  between operations  17.1 us (1%)
    unnamed x22, waiting for transfers between devices  199 us
    unnamed x3, blocking collectives  101 us
    reduce_scatter x1, waiting for transfers between devices, per_device(): lax.psum_scatter(grad_w_down, 'dp', scatter_dimension=1, tiled=True)  72.7 us
    reduce_scatter x1, waiting for transfers between devices, per_device(): lax.psum_scatter(jnp.einsum('tf,df->td', piece, full_up, preferred_elemen...  58.3 us
    reduce_scatter x1, waiting for transfers between devices, per_device(): lax.psum_scatter(jnp.dot(piece, full_down, preferred_element_type=jnp.flo...  56.8 us
    all_gather x1, waiting for transfers between devices, per_device(): lax.all_gather(grad_two.astype(jnp.bfloat16), 'tensor', axis=0, tiled=True)  46.5 us
    all_gather x1, waiting for transfers between devices, per_device(): lax.all_gather(grad_one.astype(jnp.bfloat16), 'tensor', axis=0, tiled=True)  45 us
    dot_general x8, matrix products, one_sequence(): jnp.einsum('qhd,khd->hqk', grad_block, value_one, preferred_element_type=...  43.9 us
  transfers between devices with their start and end apart: 17, of which 13 were waited for; matrix products, arithmetic and copies ran while one was open for 22% of the time, Pallas kernels for 0%

commit v1 on v0

v1 whole, which is shorter than its diff:
```python
import functools

import jax
import jax.numpy as jnp
from jax import lax
from jax.experimental import pallas as pl
from jax.experimental.pallas import tpu as pltpu
from jax.sharding import PartitionSpec as P

HD = 64
BLOCK = 256
EXTRA = 16

epsilon = 1e-06
root_half = 0.7071067811865476
inv_root_tau = 0.3989422804014327
masked_value = -1e30
bf16 = jnp.bfloat16
f32 = jnp.float32


def contract(a, b, dims, out=f32):
    return lax.dot_general(a, b, (dims, ((), ())), preferred_element_type=f32).astype(out)


def ring_order(size):
    return list(range(0, size, 2)) + list(range(size - 1, 0, -2)) if size > 1 else [0]


class Links:
    def __init__(self, dp, tensor):
        self.dp, self.tensor = dp, tensor
        order = ring_order(dp)
        self.order = jnp.array(order, jnp.int32)
        place = [0] * dp
        for position, member in enumerate(order):
            place[member] = position
        self.forward = [(order[i], order[(i + 1) % dp]) for i in range(dp)]
        self.backward = [(b, a) for a, b in self.forward]
        self.me = lax.axis_index("dp")
        self.position = jnp.array(place, jnp.int32)[self.me]
        self.ahead = dp // 2
        self.behind = dp - 1 - self.ahead

    def member(self, offset):
        return self.order[(self.position + offset + self.dp) % self.dp]

    def swap_tensor(self, value, mask):
        return lax.ppermute(value, "tensor", [(i, i ^ mask) for i in range(self.tensor)])

    def gather_ring(self, value):
        rows = value.shape[-2]
        full = jnp.zeros(value.shape[:-2] + (rows * self.dp, value.shape[-1]), value.dtype)

        def put(full, piece, offset):
            start = self.member(offset) * rows
            return lax.dynamic_update_slice_in_dim(full, piece, start, axis=full.ndim - 2)

        full = put(full, value, 0)
        up, down = value, value
        for step in range(1, self.ahead + 1):
            up = lax.ppermute(up, "dp", self.forward)
            full = put(full, up, -step)
            if step <= self.behind:
                down = lax.ppermute(down, "dp", self.backward)
                full = put(full, down, step)
        return full

    def scatter_ring(self, full):
        rows = full.shape[-2] // self.dp

        def part(offset):
            start = self.member(offset) * rows
            return lax.dynamic_slice_in_dim(full, start, rows, axis=full.ndim - 2).astype(f32)

        up = part(self.ahead).astype(bf16)
        down = part(-self.behind).astype(bf16)
        total = part(0)
        for step in range(1, self.ahead + 1):
            up = lax.ppermute(up, "dp", self.forward)
            left = self.ahead - step
            if left:
                up = (up.astype(f32) + part(left)).astype(bf16)
            else:
                total = total + up.astype(f32)
            if step <= self.behind:
                down = lax.ppermute(down, "dp", self.backward)
                left = self.behind - step
                if left:
                    down = (down.astype(f32) + part(-left)).astype(bf16)
                else:
                    total = total + down.astype(f32)
        return total

    def gather_wide(self, value):
        own = self.gather_ring(value)
        across = self.swap_tensor(own, 2)
        return (own, self.swap_tensor(own, 1), across, self.swap_tensor(across, 1))

    def gather_early(self, value):
        pair = jnp.stack([value, self.swap_tensor(value, 2)])
        pair = self.gather_ring(pair)
        other = self.swap_tensor(pair, 1)
        return (pair[0], other[0], pair[1], other[1])

    def pair_sum(self, pieces):
        one = self.swap_tensor(pieces[1].astype(bf16), 1)
        three = self.swap_tensor(pieces[3].astype(bf16), 1)
        return (pieces[0].astype(f32) + one.astype(f32), pieces[2].astype(f32) + three.astype(f32))

    def scatter_early(self, pieces):
        own, across = self.pair_sum(pieces)
        across = self.swap_tensor(across.astype(bf16), 2)
        return self.scatter_ring(own + across.astype(f32))

    def scatter_late(self, pieces):
        own, across = self.pair_sum(pieces)
        pair = self.scatter_ring(jnp.stack([own, across]).astype(bf16))
        return pair[0] + self.swap_tensor(pair[1].astype(bf16), 2).astype(f32)

    def relative(self, value):
        mine = lax.axis_index("tensor")
        low = (mine & 1) == 1
        high = (mine & 2) == 2
        value = jnp.where(low, value[:, [1, 0, 3, 2]], value)
        return jnp.where(high, value[:, [2, 3, 0, 1]], value)

    def gather_small(self, value):
        full = value[None]
        bit = 1
        while bit < self.dp:
            other = lax.ppermute(full, "dp", [(i, i ^ bit) for i in range(self.dp)])
            upper = (self.me & bit) != 0
            full = jnp.where(
                upper, jnp.concatenate([other, full]), jnp.concatenate([full, other])
            )
            bit *= 2
        across = self.swap_tensor(full, 2)
        one = self.swap_tensor(full, 1)
        three = self.swap_tensor(across, 1)
        return jnp.stack([full, one, across, three], axis=1)

    def scatter_small(self, value):
        one = self.swap_tensor(value[:, 1], 1)
        three = self.swap_tensor(value[:, 3], 1)
        own, across = value[:, 0] + one, value[:, 2] + three
        full = own + self.swap_tensor(across, 2)
        bit = self.dp // 2
        while bit:
            upper = (self.me & bit) != 0
            low, high = full[:bit], full[bit:]
            kept = jnp.where(upper, high, low)
            sent = jnp.where(upper, low, high)
            full = kept + lax.ppermute(sent, "dp", [(i, i ^ bit) for i in range(self.dp)])
            bit //= 2
        return full[0]


def attend_kernel(first_ref, last_ref, qkv_ref, seg_row_ref, seg_col_ref, out_ref, log_ref, keys, values):
    length = qkv_ref.shape[1]
    heads = qkv_ref.shape[0] // (3 * HD)
    width = heads * HD
    tail = jnp.where(lax.broadcasted_iota(jnp.int32, (EXTRA, length), 0) == 0, 1.0, 0.0).astype(bf16)
    for head in range(heads):
        rows = slice(width + head * HD, width + (head + 1) * HD)
        keys[head] = qkv_ref[rows, :].astype(f32).T.astype(bf16)
        values[head, 0:HD, :] = qkv_ref[2 * width + head * HD : 2 * width + (head + 1) * HD, :]
        values[head, HD : HD + EXTRA, :] = tail

    def one_block(block, _):
        start = pl.multiple_of(block * BLOCK, BLOCK)
        seg_query = seg_row_ref[:, pl.ds(start, BLOCK)]
        queries = [
            qkv_ref[head * HD : (head + 1) * HD, pl.ds(start, BLOCK)] * 0.125 for head in range(heads)
        ]

        def one_key(key, carry):
            offset = pl.multiple_of(key * BLOCK, BLOCK)
            allowed = seg_col_ref[pl.ds(offset, BLOCK), :] == seg_query
            result = []
            for head in range(heads):
                top, total = carry[head]
                scores = contract(keys[head, pl.ds(offset, BLOCK), :], queries[head], ((1,), (0,)))
                scores = jnp.where(allowed, scores, masked_value)
                now = jnp.maximum(top, jnp.max(scores, axis=0, keepdims=True))
                weights = jnp.exp(scores - now).astype(bf16)
                total = total * jnp.exp(top - now) + contract(
                    values[head, :, pl.ds(offset, BLOCK)], weights, ((1,), (0,))
                )
                result.append((now, total))
            return tuple(result)

        start_value = tuple(
            (
                jnp.full((1, BLOCK), masked_value, f32),
                jnp.zeros((HD + EXTRA, BLOCK), f32),
            )
            for _ in range(heads)
        )
        done = lax.fori_loop(first_ref[block], last_ref[block] + 1, one_key, start_value)
        for head in range(heads):
            top, total = done[head]
            mass = total[HD : HD + 1, :]
            out_ref[head * HD : (head + 1) * HD, pl.ds(start, BLOCK)] = (total[:HD] / mass).astype(bf16)
            log_ref[head : head + 1, pl.ds(start, BLOCK)] = top + jnp.log(mass)
        return 0

    lax.fori_loop(0, length // BLOCK, one_block, 0)


def attend(qkv, seg_row, seg_col, first, last):
    width, length = qkv.shape
    heads = width // (3 * HD)
    full = lambda *shape: pl.BlockSpec(shape, lambda i, *_: (0,) * len(shape))
    return pl.pallas_call(
        attend_kernel,
        out_shape=(
            jax.ShapeDtypeStruct((heads * HD, length), bf16),
            jax.ShapeDtypeStruct((8, length), f32),
        ),
        grid_spec=pltpu.PrefetchScalarGridSpec(
            num_scalar_prefetch=2,
            grid=(1,),
            in_specs=[full(width, length), full(1, length), full(length, 1)],
            out_specs=(full(heads * HD, length), full(8, length)),
            scratch_shapes=[
                pltpu.VMEM((heads, length, HD), bf16),
                pltpu.VMEM((heads, HD + EXTRA, length), bf16),
            ],
        ),
        cost_estimate=pl.CostEstimate(
            flops=4 * heads * length * length * HD,
            bytes_accessed=4 * width * length,
            transcendentals=heads * length * length,
        ),
        name="attend",
    )(first, last, qkv, seg_row, seg_col)


def attend_back_kernel(
    first_ref, last_ref, qkv_ref, out_ref, log_ref, grad_ref, seg_row_ref, seg_col_ref, result_ref, keys, values, delta, grad_query
):
    length = qkv_ref.shape[1]
    heads = qkv_ref.shape[0] // (3 * HD)
    width = heads * HD
    for head in range(heads):
        own = slice(head * HD, (head + 1) * HD)
        keys[head] = qkv_ref[width + head * HD : width + (head + 1) * HD, :].astype(f32).T.astype(bf16)
        values[head] = qkv_ref[2 * width + head * HD : 2 * width + (head + 1) * HD, :].astype(f32).T.astype(bf16)
        delta[head : head + 1, :] = jnp.sum(
            out_ref[own, :].astype(f32) * grad_ref[own, :].astype(f32), axis=0, keepdims=True
        )
    grad_query[...] = jnp.zeros_like(grad_query)

    def one_key(block, _):
        offset = pl.multiple_of(block * BLOCK, BLOCK)
        seg_key = seg_col_ref[pl.ds(offset, BLOCK), :]

        def one_query(query, carry):
            start = pl.multiple_of(query * BLOCK, BLOCK)
            lanes = pl.ds(start, BLOCK)
            allowed = seg_key == seg_row_ref[:, lanes]
            result = []
            for head in range(heads):
                grad_key, grad_value = carry[head]
                own = slice(head * HD, (head + 1) * HD)
                queries = qkv_ref[own, lanes] * 0.125
                grads = grad_ref[own, lanes]
                scores = contract(keys[head, pl.ds(offset, BLOCK), :], queries, ((1,), (0,)))
                scores = jnp.where(allowed, scores, masked_value)
                weights = jnp.exp(scores - log_ref[head : head + 1, lanes])
                grad_prob = contract(values[head, pl.ds(offset, BLOCK), :], grads, ((1,), (0,)))
                grad_scores = (weights * (grad_prob - delta[head : head + 1, lanes])).astype(bf16)
                grad_value = grad_value + contract(grads, weights.astype(bf16), ((1,), (1,)))
                grad_key = grad_key + contract(queries, grad_scores, ((1,), (1,)))
                key_cols = qkv_ref[width + head * HD : width + (head + 1) * HD, pl.ds(offset, BLOCK)]
                grad_query[own, lanes] += contract(key_cols, grad_scores, ((1,), (0,)))
                result.append((grad_key, grad_value))
            return tuple(result)

        zero = jnp.zeros((HD, BLOCK), f32)
        done = lax.fori_loop(
            first_ref[block], last_ref[block] + 1, one_query, tuple((zero, zero) for _ in range(heads))
        )
        for head in range(heads):
            grad_key, grad_value = done[head]
            rows = width + head * HD
            result_ref[rows : rows + HD, pl.ds(offset, BLOCK)] = grad_key.astype(bf16)
            result_ref[width + rows : width + rows + HD, pl.ds(offset, BLOCK)] = grad_value.astype(bf16)
        return 0

    lax.fori_loop(0, length // BLOCK, one_key, 0)
    result_ref[0:width, :] = (grad_query[...] * 0.125).astype(bf16)


def attend_back(qkv, out, logs, grad, seg_row, seg_col, first, last):
    width, length = qkv.shape
    heads = width // (3 * HD)
    full = lambda *shape: pl.BlockSpec(shape, lambda i, *_: (0,) * len(shape))
    return pl.pallas_call(
        attend_back_kernel,
        out_shape=jax.ShapeDtypeStruct((width, length), bf16),
        grid_spec=pltpu.PrefetchScalarGridSpec(
            num_scalar_prefetch=2,
            grid=(1,),
            in_specs=[
                full(width, length),
                full(heads * HD, length),
                full(8, length),
                full(heads * HD, length),
                full(1, length),
                full(length, 1),
            ],
            out_specs=full(width, length),
            scratch_shapes=[
                pltpu.VMEM((heads, length, HD), bf16),
                pltpu.VMEM((heads, length, HD), bf16),
                pltpu.VMEM((8, length), f32),
                pltpu.VMEM((heads * HD, length), f32),
            ],
        ),
        cost_estimate=pl.CostEstimate(
            flops=10 * heads * length * length * HD,
            bytes_accessed=6 * width * length,
            transcendentals=heads * length * length,
        ),
        name="attend_back",
    )(first, last, qkv, out, logs, grad, seg_row, seg_col)


def normalize(values, norm_gain, norm_shift):
    average = jnp.mean(values, axis=-1, keepdims=True)
    centred = values - average
    variance = jnp.mean(centred * centred, axis=-1, keepdims=True)
    inv_scale = lax.rsqrt(variance + epsilon)
    unit_rows = centred * inv_scale
    return (unit_rows * norm_gain + norm_shift, unit_rows, inv_scale)


def normalize_back(grad_out, unit_rows, inv_scale, norm_gain):
    grad_unit = grad_out * norm_gain
    middle = grad_unit - jnp.mean(grad_unit, axis=-1, keepdims=True)
    middle = middle - unit_rows * jnp.mean(grad_unit * unit_rows, axis=-1, keepdims=True)
    return inv_scale * middle


def gelu_parts(up_pre):
    normal_cdf = 0.5 * (1.0 + lax.erf(up_pre * root_half))
    return (
        up_pre * normal_cdf,
        normal_cdf + up_pre * inv_root_tau * jnp.exp(-0.5 * up_pre * up_pre),
    )


def per_device(
    tokens,
    doc_lengths,
    w_query,
    w_key,
    w_value,
    w_out,
    w_up,
    w_down,
    b_query,
    b_value,
    b_up,
    b_out,
    b_down,
    gain_one,
    shift_one,
    gain_two,
    shift_two,
    cotangent,
):
    dp, tensor = lax.axis_size("dp"), lax.axis_size("tensor")
    length, model = tokens.shape
    group = w_query.shape[1]
    hidden = w_up.shape[1]
    links = Links(dp, tensor)
    sequence = lax.axis_index("tensor")

    lengths = lax.dynamic_slice_in_dim(doc_lengths, sequence, 1, axis=0)[0]
    bounds = jnp.cumsum(lengths)
    places = jnp.arange(length, dtype=jnp.int32)
    segment = jnp.sum((bounds[None, :] <= places[:, None]).astype(jnp.int32), axis=-1)
    seg_row, seg_col = segment[None, :], segment[:, None]
    blocks = segment.reshape(-1, BLOCK)
    low, high = blocks[:, 0], blocks[:, -1]
    meets = (low[:, None] <= high[None, :]) & (low[None, :] <= high[:, None])
    count = low.shape[0]
    index = jnp.arange(count, dtype=jnp.int32)
    first = jnp.min(jnp.where(meets, index[None, :], count), axis=1)
    last = jnp.max(jnp.where(meets, index[None, :], -1), axis=1)

    vectors = (b_out, b_down, gain_one, shift_one, gain_two, shift_two)
    share = b_out.shape[0]
    small = jnp.concatenate(
        list(vectors) + [v.astype(f32).reshape(-1) for v in (b_query, b_value, b_up)]
    )
    used = small.shape[0]
    small = jnp.pad(small, (0, -used % 128))
    small = links.gather_small(small)
    flat = links.relative(small)[:, :, : 6 * share].reshape(dp * tensor, 6, share)
    flat = flat.transpose(1, 0, 2).reshape(6, model)
    bias_out, bias_down, norm_gain_one, norm_shift_one, norm_gain_two, norm_shift_two = flat
    heads = b_query.shape[0]
    taken = 6 * share

    def columns(rows, per):
        nonlocal taken
        part = small[:, :, taken : taken + rows * per].reshape(dp, tensor, rows, per)
        taken += rows * per
        return part.transpose(1, 2, 0, 3).reshape(tensor, -1)

    bias_query = columns(heads, b_query.shape[1])
    bias_value = columns(heads, b_value.shape[1])
    bias_up = columns(b_up.shape[0], b_up.shape[1])

    attn_w = links.gather_early(jnp.concatenate([w_query, w_key, w_value, w_out.T], axis=1))
    up_w = links.gather_wide(w_up)
    down_w = links.gather_early(w_down.T)

    qkv, mixture, logs = [], [], []
    for j in range(tensor):
        bias = jnp.concatenate([bias_query[j], jnp.zeros((group,), f32), bias_value[j]])
        made = contract(attn_w[j][:, : 3 * group], tokens, ((0,), (1,))) + bias[:, None]
        qkv.append(made.astype(bf16))
        mixed, log = attend(qkv[j], seg_row, seg_col, first, last)
        mixture.append(mixed)
        logs.append(log)
    attn = bias_out + tokens.astype(f32)
    for j in range(tensor):
        attn = attn + contract(mixture[j], attn_w[j][:, 3 * group :], ((0,), (1,)))
    first_out, unit_one, scale_one = normalize(attn, norm_gain_one, norm_shift_one)
    first_low = first_out.astype(bf16)
    activated, slopes = [], []
    for j in range(tensor):
        up_pre = contract(first_low, up_w[j], ((1,), (0,))) + bias_up[j]
        act, slope = gelu_parts(up_pre)
        activated.append(act.astype(bf16))
        slopes.append(slope.astype(bf16))
    residual = bias_down + first_out
    for j in range(tensor):
        residual = residual + contract(activated[j], down_w[j], ((1,), (1,)))
    result, unit_two, scale_two = normalize(residual, norm_gain_two, norm_shift_two)
    grad_out = cotangent.astype(f32)
    grad_two = normalize_back(grad_out, unit_two, scale_two, norm_gain_two)
    grad_gain_two = jnp.sum(grad_out * unit_two, axis=0)
    grad_shift_two = jnp.sum(grad_out, axis=0)
    grad_bias_down = jnp.sum(grad_two, axis=0)
    grad_two_low = grad_two.astype(bf16)
    grad_down = [contract(grad_two_low, activated[j], ((0,), (0,)), bf16) for j in range(tensor)]
    grad_down = links.scatter_late(grad_down)
    grad_up, grad_w_up, grad_bias_up = [], [], []
    grad_first = grad_two
    for j in range(tensor):
        made = contract(grad_two_low, down_w[j], ((1,), (0,))) * slopes[j].astype(f32)
        grad_up.append(made.astype(bf16))
        grad_bias_up.append(jnp.sum(grad_up[j].astype(f32), axis=0))
        grad_w_up.append(contract(first_low, grad_up[j], ((0,), (0,)), bf16))
        grad_first = grad_first + contract(grad_up[j], up_w[j], ((1,), (1,)))
    grad_w_up = links.scatter_early(grad_w_up)
    grad_one = normalize_back(grad_first, unit_one, scale_one, norm_gain_one)
    grad_gain_one = jnp.sum(grad_first * unit_one, axis=0)
    grad_shift_one = jnp.sum(grad_first, axis=0)
    grad_bias_out = jnp.sum(grad_one, axis=0)
    grad_one_low = grad_one.astype(bf16)
    grad_attn, grad_bias_query, grad_bias_value = [], [], []
    grad_input = grad_one
    for j in range(tensor):
        grad_mix = contract(attn_w[j][:, 3 * group :], grad_one_low, ((0,), (1,)), bf16)
        grad_qkv = attend_back(qkv[j], mixture[j], logs[j], grad_mix, seg_row, seg_col, first, last)
        sums = jnp.sum(grad_qkv.astype(f32), axis=1)
        grad_bias_query.append(sums[:group])
        grad_bias_value.append(sums[2 * group :])
        grad_attn.append(
            jnp.concatenate(
                [
                    contract(tokens, grad_qkv, ((0,), (1,)), bf16),
                    contract(grad_one_low, mixture[j], ((0,), (1,)), bf16),
                ],
                axis=1,
            )
        )
        grad_input = grad_input + contract(grad_qkv, attn_w[j][:, : 3 * group], ((0,), (1,)))
    grad_attn = links.scatter_late(grad_attn)

    sums = jnp.stack(
        [grad_bias_out, grad_bias_down, grad_gain_one, grad_shift_one, grad_gain_two, grad_shift_two]
    )
    sums = sums.reshape(6, dp, tensor, share).transpose(1, 2, 0, 3).reshape(dp, tensor, 6 * share)
    sums = links.relative(sums)

    def spread(pieces, rows, per):
        stacked = jnp.stack(pieces).reshape(tensor, rows, dp, per)
        return stacked.transpose(2, 0, 1, 3).reshape(dp, tensor, rows * per)

    shapes = [b_query.shape, b_value.shape, b_up.shape]
    sums = jnp.concatenate(
        [sums]
        + [
            spread(pieces, *shape)
            for pieces, shape in zip((grad_bias_query, grad_bias_value, grad_bias_up), shapes)
        ],
        axis=2,
    )
    sums = jnp.pad(sums, ((0, 0), (0, 0), (0, -used % 128)))
    sums = links.scatter_small(sums)
    vector_sums = [sums[i * share : (i + 1) * share] for i in range(6)]
    at = 6 * share
    tables = []
    for rows, per in shapes:
        tables.append(sums[at : at + rows * per].reshape(rows, per))
        at += rows * per
    return (
        result.astype(bf16),
        grad_input.astype(bf16),
        grad_attn[:, :group],
        grad_attn[:, group : 2 * group],
        grad_attn[:, 2 * group : 3 * group],
        grad_attn[:, 3 * group :].T,
        grad_w_up,
        grad_down.T,
        *tables,
        *vector_sums,
    )


def solution(mesh):
    both = P(("dp", "tensor"))
    rows = P(("dp", "tensor"), None)
    down = P("tensor", "dp")
    wide = P("dp", "tensor")
    weights = (wide, wide, wide, down, wide, down, down, down, down)
    return jax.shard_map(
        per_device,
        mesh=mesh,
        in_specs=(rows, P("dp", None)) + weights + (both,) * 6 + (rows,),
        out_specs=(rows, rows) + weights + (both,) * 6,
        check_vma=False,
    )
```

time: 1360 us -> 573 us (0.42)
  waiting for transfers between devices: 597 us -> 72.7 us
  blocking collectives: 295 us -> 0 us
  Pallas kernels: 0 us -> 118 us
  matrix products: 276 us -> 159 us
  starting transfers between devices: 0.9 us -> 70.8 us
  other arithmetic: 88.6 us -> 33.3 us
  local copies, waits for them, and re-layouts: 73.7 us -> 93.9 us
    reduce_scatter x6 -> x0, waiting for transfers between devices: 257 us -> none  [the longest x1 72.7 us: per_device(): lax.psum_scatter(grad_w_down, 'dp', scatter_dimension=1, tiled=True)]
    unnamed x22 -> x0, waiting for transfers between devices: 199 us -> none
    all_gather x7 -> x0, blocking collectives: 194 us -> none  [the longest x1 33.3 us: per_device(): lax.all_gather(w_key, 'dp', axis=0, tiled=True)]
    all_gather x6 -> x0, waiting for transfers between devices: 141 us -> none  [the longest x1 46.5 us: per_device(): lax.all_gather(grad_two.astype(jnp.bfloat16), 'tensor', axis=0, tiled=True)]
    pallas_call x0 -> x8, Pallas kernels: none -> 118 us  [the longest x4 60.6 us: attend_back(): pl.pallas_call(attend_back_kernel, out_shape=jax.ShapeDtypeStruct((width,...]
    dot_general x73 -> x48, matrix products: 272 us -> 159 us  [contract(): lax.dot_general(a, b, (dims, ((), ())), preferred_element_type=f32)]
    unnamed x3 -> x0, blocking collectives: 101 us -> none
    ppermute x0 -> x70, waiting for transfers between devices: none -> 72.7 us  [the longest x12 26.6 us: scatter_ring(): up = lax.ppermute(up, 'dp', self.forward)]
  transfers between devices with their start and end apart: 17 -> 70, of which waited for: 13 -> 24; matrix products, arithmetic and copies ran while one was open for 22% -> 30% of each run, Pallas kernels for 0% -> 10%
where the time goes in v1:
time: 573 us; the launch traced here: 562 us
  matrix products  159 us (28%)
  Pallas kernels  118 us (21%)
  local copies, waits for them, and re-layouts  93.9 us (16%)
  waiting for transfers between devices  72.7 us (13%)
  starting transfers between devices  70.8 us (12%)
  other arithmetic  33.3 us (6%)
  between operations  14.3 us (2%)
    dot_general x48, matrix products, contract(): lax.dot_general(a, b, (dims, ((), ())), preferred_element_type=f32)  159 us
    pallas_call x4, Pallas kernels, attend_back(): pl.pallas_call(attend_back_kernel, out_shape=jax.ShapeDtypeStruct((width,...  60.6 us
    pallas_call x4, Pallas kernels, attend(): pl.pallas_call(attend_kernel, out_shape=(jax.ShapeDtypeStruct((heads * HD...  57.4 us
    dynamic_update_slice x23, local copies, waits for them, and re-layouts, put(): lax.dynamic_update_slice_in_dim(full, piece, start, axis=full.ndim - 2)  30.6 us
    ppermute x12, waiting for transfers between devices, scatter_ring(): up = lax.ppermute(up, 'dp', self.forward)  26.6 us
    ppermute x12, starting transfers between devices, scatter_ring(): up = lax.ppermute(up, 'dp', self.forward)  20.5 us
    ppermute x12, starting transfers between devices, gather_ring(): up = lax.ppermute(up, 'dp', self.forward)  20.1 us
    ppermute x12, waiting for transfers between devices, gather_ring(): up = lax.ppermute(up, 'dp', self.forward)  19.5 us
  transfers between devices with their start and end apart: 70, of which 24 were waited for; matrix products, arithmetic and copies ran while one was open for 30% of the time, Pallas kernels for 10%

profile of v1, /device:TPU:0, one launch (start us, length us, event | category | flops | bytes accessed | tf_op | source)
XLA Modules:
  0.0 562.1 jit_solution(15272339431639460763)
XLA Ops:
  0.7 3.1 collective-permute-start.15
  30.3 2.7 collective-permute-start.2
  78.4 6.0 %collective-permute-done.17 = bf16[96,768]{1,0:T(8,128)(2,1)} collective-permute-done((bf16[96,768]{1,0:T(8,128)(2,1)}, bf16[96,768]{1,0:T(8,128)(2,1)}, u32[]{:S(2)}, u32[]{:S(2)}) %collective-permute-start.17) | collective-permute-done | bytes 147488 | tf_op jit(solution)/shard_map/ppermute | solution.py:62
  112.4 5.8 %collective-permute-done.21 = bf16[96,768]{1,0:T(8,128)(2,1)S(1)} collective-permute-done((bf16[96,768]{1,0:T(8,128)(2,1)}, bf16[96,768]{1,0:T(8,128)(2,1)S(1)}, u32[]{:S(2)}, u32[]{:S(2)}) %collective-permute-start.21) | collective-permute-done | bytes 147488 | tf_op jit(solution)/shard_map/ppermute | solution.py:62
  151.0 2.9 slice_bitcast_fusion.7
  156.2 14.7 %attend.4 = (bf16[192,1024]{1,0:T(8,128)(2,1)}, f32[8,1024]{1,0:T(8,128)}) custom-call(s32[4]{0:T(128)} %get-tuple-element.121.first_ref, s32[4]{0:T(128)} %get-tuple-element.120.last_ref, bf16[576,1024]{1,0:T(8,128)(2,1)} %add_convert_fusion.10.qkv_ref, s32[1,1024]{1,0:T(1,128)} %bitcast.272, s32[1024,1]{1,0:T(8,128)} %copy.203.seg_col_ref), custom_call_target="tpu_custom_call" | custom-call | flops 805306368 | bytes 2359296 | tf_op jit(solution)/shard_map/attend/pallas_call | solution.py:215
  171.0 4.0 add_convert_fusion.8.qkv_ref
  174.9 14.3 %attend.6 = (bf16[192,1024]{1,0:T(8,128)(2,1)}, f32[8,1024]{1,0:T(8,128)}) custom-call(s32[4]{0:T(128)} %get-tuple-element.121.first_ref, s32[4]{0:T(128)} %get-tuple-element.120.last_ref, bf16[576,1024]{1,0:T(8,128)(2,1)} %add_convert_fusion.8.qkv_ref, s32[1,1024]{1,0:T(1,128)} %bitcast.273, s32[1024,1]{1,0:T(8,128)} %copy.203.seg_col_ref), custom_call_target="tpu_custom_call" | custom-call | flops 805306368 | bytes 2359296 | tf_op jit(solution)/shard_map/attend/pallas_call | solution.py:215
  189.2 3.4 fusion.65
  192.6 3.3 fusion.59
  195.9 3.0 slice_bitcast_fusion.4
  202.2 14.1 %attend.5 = (bf16[192,1024]{1,0:T(8,128)(2,1)}, f32[8,1024]{1,0:T(8,128)}) custom-call(s32[4]{0:T(128)} %get-tuple-element.121.first_ref, s32[4]{0:T(128)} %get-tuple-element.120.last_ref, bf16[576,1024]{1,0:T(8,128)(2,1)} %add_convert_fusion.9.qkv_ref, s32[1,1024]{1,0:T(1,128)} %bitcast.274, s32[1024,1]{1,0:T(8,128)} %copy.203.seg_col_ref), custom_call_target="tpu_custom_call" | custom-call | flops 805306368 | bytes 2359296 | tf_op jit(solution)/shard_map/attend/pallas_call | solution.py:215
  216.4 3.6 fusion.62
  222.3 14.3 %attend.7 = (bf16[192,1024]{1,0:T(8,128)(2,1)}, f32[8,1024]{1,0:T(8,128)}) custom-call(s32[4]{0:T(128)} %get-tuple-element.121.first_ref, s32[4]{0:T(128)} %get-tuple-element.120.last_ref, bf16[576,1024]{1,0:T(8,128)(2,1)} %add_convert_fusion.7.qkv_ref, s32[1,1024]{1,0:T(1,128)} %bitcast.275, s32[1024,1]{1,0:T(8,128)} %copy.203.seg_col_ref), custom_call_target="tpu_custom_call" | custom-call | flops 805306368 | bytes 2359296 | tf_op jit(solution)/shard_map/attend/pallas_call | solution.py:215
  236.6 5.1 fusion.101
  242.8 4.0 multiply_convert_fusion.7
  246.7 3.3 fusion.32
  250.0 2.7 fusion.103
  252.8 5.2 multiply_convert_fusion.6
  258.0 3.3 fusion.33
  261.3 4.4 multiply_convert_fusion.4
  265.7 3.3 fusion.35
  269.0 3.6 fusion.102
  273.9 3.8 fusion.6
  277.6 5.1 convert_reduce_fusion.2
  282.7 5.4 convert_reduce_fusion.4
  288.1 4.5 convert_reduce_fusion.3
  292.6 3.3 fusion.104
  295.9 2.8 fusion.105
  298.7 4.5 convert_reduce_fusion.1
  303.2 3.2 fusion.106
  306.5 6.2 %multiply_reduce_fusion = (f32[768]{0:T(1024)}, f32[1024]{0:T(1024)S(1)}, f32[1024]{0:T(1024)S(1)}, f32[768]{0:T(1024)S(1)}, f32[1024,768]{0,1:T(8,128)S(1)}) fusion(f32[1024,768]{0,1:T(8,128)S(1)} %get-tuple-element.198, f32[1024]{0:T(1024)S(1)} %add_rsqrt_fusion.1, f32[1024]{0:T(1024)S(1)} %broadcast_multiply_fusion.5, f32[768]{0:T(1024)S(1)} %mul.302, ...), kind=kOutput, calls=%fused_computation.70 | convolution fusion | flops 1224471040 | bytes 23244800 | tf_op jit(solution)/shard_map/dot_general | solution.py:23
  314.0 2.6 convolution_convert_fusion.12.grad_ref
  316.7 2.3 convolution_convert_fusion.15.grad_ref
  319.0 2.5 convolution_convert_fusion.14.grad_ref
  321.5 2.3 convolution_convert_fusion.13.grad_ref
  323.8 2.4 convolution_convert_fusion
  326.3 2.4 convolution_convert_fusion.2
  328.7 2.4 convolution_convert_fusion.7
  331.1 2.4 convolution_convert_fusion.6
  333.6 2.5 convolution_convert_fusion.4
  337.4 15.1 %attend_back.7 = bf16[576,1024]{1,0:T(8,128)(2,1)} custom-call(s32[4]{0:T(128)} %get-tuple-element.121.first_ref, s32[4]{0:T(128)} %get-tuple-element.120.last_ref, bf16[576,1024]{1,0:T(8,128)(2,1)} %add_convert_fusion.7.qkv_ref, bf16[192,1024]{1,0:T(8,128)(2,1)} %get-tuple-element.28.out_ref, f32[8,1024]{1,0:T(8,128)} %get-tuple-element.32.log_ref, ...), custom_call_target="tpu_custom_call" | custom-call | flops 2013265920 | bytes 3538944 | tf_op jit(solution)/shard_map/attend_back/pallas_call | solution.py:300
  354.1 3.8 fusion.27
  357.9 15.3 %attend_back.6 = bf16[576,1024]{1,0:T(8,128)(2,1)} custom-call(s32[4]{0:T(128)} %get-tuple-element.121.first_ref, s32[4]{0:T(128)} %get-tuple-element.120.last_ref, bf16[576,1024]{1,0:T(8,128)(2,1)} %add_convert_fusion.8.qkv_ref, bf16[192,1024]{1,0:T(8,128)(2,1)} %get-tuple-element.27.out_ref, f32[8,1024]{1,0:T(8,128)} %get-tuple-element.31.log_ref, ...), custom_call_target="tpu_custom_call" | custom-call | flops 2013265920 | bytes 3538944 | tf_op jit(solution)/shard_map/attend_back/pallas_call | solution.py:300
  374.7 3.8 fusion.26
  378.5 15.1 %attend_back.5 = bf16[576,1024]{1,0:T(8,128)(2,1)} custom-call(s32[4]{0:T(128)} %get-tuple-element.121.first_ref, s32[4]{0:T(128)} %get-tuple-element.120.last_ref, bf16[576,1024]{1,0:T(8,128)(2,1)} %add_convert_fusion.9.qkv_ref, bf16[192,1024]{1,0:T(8,128)(2,1)} %get-tuple-element.26.out_ref, f32[8,1024]{1,0:T(8,128)} %get-tuple-element.30.log_ref, ...), custom_call_target="tpu_custom_call" | custom-call | flops 2013265920 | bytes 3538944 | tf_op jit(solution)/shard_map/attend_back/pallas_call | solution.py:300
  395.1 3.8 fusion.25
  398.9 15.1 %attend_back.4 = bf16[576,1024]{1,0:T(8,128)(2,1)} custom-call(s32[4]{0:T(128)} %get-tuple-element.121.first_ref, s32[4]{0:T(128)} %get-tuple-element.120.last_ref, bf16[576,1024]{1,0:T(8,128)(2,1)} %add_convert_fusion.10.qkv_ref, bf16[192,1024]{1,0:T(8,128)(2,1)} %get-tuple-element.25.out_ref, f32[8,1024]{1,0:T(8,128)} %get-tuple-element.29.log_ref, ...), custom_call_target="tpu_custom_call" | custom-call | flops 2013265920 | bytes 3538944 | tf_op jit(solution)/shard_map/attend_back/pallas_call | solution.py:300
  415.5 3.9 fusion.24
  419.4 3.1 fusion.44
  422.5 3.1 fusion.41
  425.7 3.2 fusion.38
  433.9 7.3 %add_convert_fusion = bf16[1024,768]{0,1:T(8,128)(2,1)} fusion(f32[1024,768]{0,1:T(8,128)} %fusion.38, f32[1024,768]{0,1:T(8,128)} %fusion.41, f32[1024,768]{0,1:T(8,128)S(1)} %get-tuple-element.123, f32[1024,768]{0,1:T(8,128)} %fusion.44, bf16[576,1024]{1,0:T(8,128)(2,1)} %attend_back.7, bf16[768,768]{1,0:T(8,128)(2,1)} %get-tuple-element.140), kind=kOutput, calls=%fused_computation.71 | convolution fusion | flops 909901824 | bytes 16318464 | tf_op jit(solution)/shard_map/dot_general | solution.py:23
  445.7 2.9 collective-permute-start.67
  460.8 3.7 fusion.29
  464.5 2.7 fusion.28
  472.1 3.7 add_convert_fusion.4
  479.0 5.8 %collective-permute-done.36 = bf16[2,96,768]{1,2,0:T(8,128)(2,1)S(1)} collective-permute-done((bf16[2,96,768]{1,2,0:T(8,128)(2,1)S(1)}, bf16[2,96,768]{1,2,0:T(8,128)(2,1)S(1)}, u32[]{:S(2)}, u32[]{:S(2)}) %collective-permute-start.36) | collective-permute-done | bytes 294944 | tf_op jit(solution)/shard_map/ppermute | solution.py:87
  487.5 7.3 %collective-permute-done.57 = bf16[2,96,768]{2,1,0:T(8,128)(2,1)S(1)} collective-permute-done((bf16[2,96,768]{2,1,0:T(8,128)(2,1)S(1)}, bf16[2,96,768]{2,1,0:T(8,128)(2,1)S(1)}, u32[]{:S(2)}, u32[]{:S(2)}) %collective-permute-start.57) | collective-permute-done | bytes 294944 | tf_op jit(solution)/shard_map/ppermute | solution.py:87
  497.4 4.1 collective-permute-done.37
  508.5 4.3 collective-permute-done.40
  523.3 8.3 %collective-permute-done.50 = bf16[96,768]{1,0:T(8,128)(2,1)S(1)} collective-permute-done((bf16[96,768]{1,0:T(8,128)(2,1)S(1)}, bf16[96,768]{1,0:T(8,128)(2,1)S(1)}, u32[]{:S(2)}, u32[]{:S(2)}) %collective-permute-start.50) | collective-permute-done | bytes 147488 | tf_op jit(solution)/shard_map/ppermute | solution.py:80
  536.7 8.0 %collective-permute-done.51 = bf16[96,768]{1,0:T(8,128)(2,1)S(1)} collective-permute-done((bf16[96,768]{1,0:T(8,128)(2,1)S(1)}, bf16[96,768]{1,0:T(8,128)(2,1)S(1)}, u32[]{:S(2)}, u32[]{:S(2)}) %collective-permute-start.51) | collective-permute-done | bytes 147488 | tf_op jit(solution)/shard_map/ppermute | solution.py:80
  547.8 2.7 collective-permute-done.42
  (521 shorter events, 211.2 us)
Async XLA Ops:
  0.7 70.2 %collective-permute-start.15 = (bf16[96,768]{1,0:T(8,128)(2,1)}, bf16[96,768]{1,0:T(8,128)(2,1)}, u32[]{:S(2)}, u32[]{:S(2)}) collective-permute-start(bf16[96,768]{1,0:T(8,128)(2,1)} %param.30), channel_id=1, source_target_pairs={{0,8},{8,16},{16,24},{24,28},{28,20},{20,12},{12,4},{4,0},{1,9},{9... | collective-permute-start | bytes 442376 | tf_op jit(solution)/shard_map/ppermute | solution.py:62
  3.8 71.1 %collective-permute-start.16 = (bf16[96,768]{1,0:T(8,128)(2,1)}, bf16[96,768]{1,0:T(8,128)(2,1)}, u32[]{:S(2)}, u32[]{:S(2)}) collective-permute-start(bf16[96,768]{1,0:T(8,128)(2,1)} %param.30), channel_id=1, source_target_pairs={{8,0},{16,8},{24,16},{28,24},{20,28},{12,20},{4,12},{0,4},{9,1},{1... | collective-permute-start | bytes 442376 | tf_op jit(solution)/shard_map/ppermute | solution.py:65
  8.2 53.8 %collective-permute-start.6 = (bf16[96,768]{0,1:T(8,128)(2,1)}, bf16[96,768]{0,1:T(8,128)(2,1)}, u32[]{:S(2)}, u32[]{:S(2)}) collective-permute-start(bf16[96,768]{0,1:T(8,128)(2,1)} %get-tuple-element.151), channel_id=1, source_target_pairs={{0,2},{1,3},{2,0},{3,1},{4,6},{5,7},{6,4},{7,5},{8,10},{9,11},{10,... | collective-permute-start | bytes 442376 | tf_op jit(solution)/shard_map/ppermute | solution.py:49
  13.2 13.4 %collective-permute-start = (f32[1,384]{1,0:T(1,128)S(1)}, f32[1,384]{1,0:T(1,128)S(1)}, u32[]{:S(2)}, u32[]{:S(2)}) collective-permute-start(f32[1,384]{1,0:T(1,128)S(1)} %broadcast_in_dim.60), channel_id=1, source_target_pairs={{0,4},{4,0},{8,12},{12,8},{16,20},{20,16},{24,28},{28,24},{1,5},{5... | collective-permute-start | bytes 4616 | tf_op jit(solution)/shard_map/ppermute | solution.py:132
  30.3 4.6 collective-permute-start.2
  35.0 9.5 %collective-permute-start.4 = (f32[8,384]{1,0:T(8,128)S(1)}, f32[8,384]{1,0:T(8,128)S(1)}, u32[]{:S(2)}, u32[]{:S(2)}) collective-permute-start(f32[8,384]{1,0:T(8,128)S(1)} %maximum_select_fusion.1), channel_id=1, source_target_pairs={{0,2},{1,3},{2,0},{3,1},{4,6},{5,7},{6,4},{7,5},{8,10},{9,11},{10,... | collective-permute-start | bytes 36872 | tf_op jit(solution)/shard_map/ppermute | solution.py:49
  45.6 20.4 %collective-permute-start.22 = (bf16[96,768]{1,0:T(8,128)(2,1)}, bf16[96,768]{1,0:T(8,128)(2,1)}, u32[]{:S(2)}, u32[]{:S(2)}) collective-permute-start(bf16[96,768]{1,0:T(8,128)(2,1)} %bitcast.37), channel_id=1, source_target_pairs={{0,2},{1,3},{2,0},{3,1},{4,6},{5,7},{6,4},{7,5},{8,10},{9,11},{10,... | collective-permute-start | bytes 442376 | tf_op jit(solution)/shard_map/ppermute | solution.py:49
  64.0 25.7 %collective-permute-start.7 = (bf16[2,96,768]{1,2,0:T(8,128)(2,1)S(1)}, bf16[2,96,768]{1,2,0:T(8,128)(2,1)S(1)}, u32[]{:S(2)}, u32[]{:S(2)}) collective-permute-start(bf16[2,96,768]{1,2,0:T(8,128)(2,1)S(1)} %pad_maximum_fusion.2), channel_id=1, source_target_pairs={{0,8},{8,16},{16,24},{24,28},{28,20},{20,12},{12,4},{4,0},{1,9},{9... | collective-permute-start | bytes 884744 | tf_op jit(solution)/shard_map/ppermute | solution.py:62
  65.5 29.0 %collective-permute-start.8 = (bf16[2,96,768]{1,2,0:T(8,128)(2,1)S(1)}, bf16[2,96,768]{1,2,0:T(8,128)(2,1)}, u32[]{:S(2)}, u32[]{:S(2)}) collective-permute-start(bf16[2,96,768]{1,2,0:T(8,128)(2,1)S(1)} %pad_maximum_fusion.2), channel_id=1, source_target_pairs={{8,0},{16,8},{24,16},{28,24},{20,28},{12,20},{4,12},{0,4},{9,1},{1... | collective-permute-start | bytes 884744 | tf_op jit(solution)/shard_map/ppermute | solution.py:65
  69.4 28.5 %collective-permute-start.23 = (bf16[2,96,768]{2,1,0:T(8,128)(2,1)}, bf16[2,96,768]{2,1,0:T(8,128)(2,1)}, u32[]{:S(2)}, u32[]{:S(2)}) collective-permute-start(bf16[2,96,768]{2,1,0:T(8,128)(2,1)} %get-tuple-element.148), channel_id=1, source_target_pairs={{0,8},{8,16},{16,24},{24,28},{28,20},{20,12},{12,4},{4,0},{1,9},{9... | collective-permute-start | bytes 884744 | tf_op jit(solution)/shard_map/ppermute | solution.py:62
  71.0 13.5 %collective-permute-start.17 = (bf16[96,768]{1,0:T(8,128)(2,1)}, bf16[96,768]{1,0:T(8,128)(2,1)}, u32[]{:S(2)}, u32[]{:S(2)}) collective-permute-start(bf16[96,768]{1,0:T(8,128)(2,1)} %collective-permute-done.15), channel_id=1, source_target_pairs={{0,8},{8,16},{16,24},{24,28},{28,20},{20,12},{12,4},{4,0},{1,9},{9... | collective-permute-start | bytes 442376 | tf_op jit(solution)/shard_map/ppermute | solution.py:62
  74.9 11.7 %collective-permute-start.18 = (bf16[96,768]{1,0:T(8,128)(2,1)}, bf16[96,768]{1,0:T(8,128)(2,1)}, u32[]{:S(2)}, u32[]{:S(2)}) collective-permute-start(bf16[96,768]{1,0:T(8,128)(2,1)} %collective-permute-done.16), channel_id=1, source_target_pairs={{8,0},{16,8},{24,16},{28,24},{20,28},{12,20},{4,12},{0,4},{9,1},{1... | collective-permute-start | bytes 442376 | tf_op jit(solution)/shard_map/ppermute | solution.py:65
  84.5 17.2 %collective-permute-start.24 = (bf16[2,96,768]{2,1,0:T(8,128)(2,1)}, bf16[2,96,768]{2,1,0:T(8,128)(2,1)}, u32[]{:S(2)}, u32[]{:S(2)}) collective-permute-start(bf16[2,96,768]{2,1,0:T(8,128)(2,1)} %get-tuple-element.148), channel_id=1, source_target_pairs={{8,0},{16,8},{24,16},{28,24},{20,28},{12,20},{4,12},{0,4},{9,1},{1... | collective-permute-start | bytes 884744 | tf_op jit(solution)/shard_map/ppermute | solution.py:65
  86.5 13.6 %collective-permute-start.19 = (bf16[96,768]{1,0:T(8,128)(2,1)}, bf16[96,768]{1,0:T(8,128)(2,1)}, u32[]{:S(2)}, u32[]{:S(2)}) collective-permute-start(bf16[96,768]{1,0:T(8,128)(2,1)} %collective-permute-done.17), channel_id=1, source_target_pairs={{0,8},{8,16},{16,24},{24,28},{28,20},{20,12},{12,4},{4,0},{1,9},{9... | collective-permute-start | bytes 442376 | tf_op jit(solution)/shard_map/ppermute | solution.py:62
  90.4 16.1 %collective-permute-start.20 = (bf16[96,768]{1,0:T(8,128)(2,1)}, bf16[96,768]{1,0:T(8,128)(2,1)}, u32[]{:S(2)}, u32[]{:S(2)}) collective-permute-start(bf16[96,768]{1,0:T(8,128)(2,1)} %collective-permute-done.18), channel_id=1, source_target_pairs={{8,0},{16,8},{24,16},{28,24},{20,28},{12,20},{4,12},{0,4},{9,1},{1... | collective-permute-start | bytes 442376 | tf_op jit(solution)/shard_map/ppermute | solution.py:65
  96.4 12.4 %collective-permute-start.9 = (bf16[2,96,768]{1,2,0:T(8,128)(2,1)}, bf16[2,96,768]{1,2,0:T(8,128)(2,1)}, u32[]{:S(2)}, u32[]{:S(2)}) collective-permute-start(bf16[2,96,768]{1,2,0:T(8,128)(2,1)} %copy-done.34), channel_id=1, source_target_pairs={{0,8},{8,16},{16,24},{24,28},{28,20},{20,12},{12,4},{4,0},{1,9},{9... | collective-permute-start | bytes 884744 | tf_op jit(solution)/shard_map/ppermute | solution.py:62
  97.9 13.9 %collective-permute-start.10 = (bf16[2,96,768]{1,2,0:T(8,128)(2,1)}, bf16[2,96,768]{1,2,0:T(8,128)(2,1)}, u32[]{:S(2)}, u32[]{:S(2)}) collective-permute-start(bf16[2,96,768]{1,2,0:T(8,128)(2,1)} %collective-permute-done.8), channel_id=1, source_target_pairs={{8,0},{16,8},{24,16},{28,24},{20,28},{12,20},{4,12},{0,4},{9,1},{1... | collective-permute-start | bytes 884744 | tf_op jit(solution)/shard_map/ppermute | solution.py:65
  100.1 27.1 %collective-permute-start.25 = (bf16[2,96,768]{2,1,0:T(8,128)(2,1)}, bf16[2,96,768]{2,1,0:T(8,128)(2,1)}, u32[]{:S(2)}, u32[]{:S(2)}) collective-permute-start(bf16[2,96,768]{2,1,0:T(8,128)(2,1)} %collective-permute-done.23), channel_id=1, source_target_pairs={{0,8},{8,16},{16,24},{24,28},{28,20},{20,12},{12,4},{4,0},{1,9},{9... | collective-permute-start | bytes 884744 | tf_op jit(solution)/shard_map/ppermute | solution.py:62
  101.7 16.5 %collective-permute-start.21 = (bf16[96,768]{1,0:T(8,128)(2,1)}, bf16[96,768]{1,0:T(8,128)(2,1)S(1)}, u32[]{:S(2)}, u32[]{:S(2)}) collective-permute-start(bf16[96,768]{1,0:T(8,128)(2,1)} %collective-permute-done.19), channel_id=1, source_target_pairs={{0,8},{8,16},{16,24},{24,28},{28,20},{20,12},{12,4},{4,0},{1,9},{9... | collective-permute-start | bytes 442376 | tf_op jit(solution)/shard_map/ppermute | solution.py:62
  106.5 21.6 %collective-permute-start.26 = (bf16[2,96,768]{2,1,0:T(8,128)(2,1)}, bf16[2,96,768]{2,1,0:T(8,128)(2,1)}, u32[]{:S(2)}, u32[]{:S(2)}) collective-permute-start(bf16[2,96,768]{2,1,0:T(8,128)(2,1)} %collective-permute-done.24), channel_id=1, source_target_pairs={{8,0},{16,8},{24,16},{28,24},{20,28},{12,20},{4,12},{0,4},{9,1},{1... | collective-permute-start | bytes 884744 | tf_op jit(solution)/shard_map/ppermute | solution.py:65
  108.8 15.1 %collective-permute-start.11 = (bf16[2,96,768]{1,2,0:T(8,128)(2,1)}, bf16[2,96,768]{1,2,0:T(8,128)(2,1)}, u32[]{:S(2)}, u32[]{:S(2)}) collective-permute-start(bf16[2,96,768]{1,2,0:T(8,128)(2,1)} %collective-permute-done.9), channel_id=1, source_target_pairs={{0,8},{8,16},{16,24},{24,28},{28,20},{20,12},{12,4},{4,0},{1,9},{9... | collective-permute-start | bytes 884744 | tf_op jit(solution)/shard_map/ppermute | solution.py:62
  111.9 17.7 %collective-permute-start.12 = (bf16[2,96,768]{1,2,0:T(8,128)(2,1)}, bf16[2,96,768]{1,2,0:T(8,128)(2,1)}, u32[]{:S(2)}, u32[]{:S(2)}) collective-permute-start(bf16[2,96,768]{1,2,0:T(8,128)(2,1)} %collective-permute-done.10), channel_id=1, source_target_pairs={{8,0},{16,8},{24,16},{28,24},{20,28},{12,20},{4,12},{0,4},{9,1},{1... | collective-permute-start | bytes 884744 | tf_op jit(solution)/shard_map/ppermute | solution.py:65
  118.8 134.0 %collective-permute-start.30 = (bf16[768,768]{1,0:T(8,128)(2,1)}, bf16[768,768]{1,0:T(8,128)(2,1)}, u32[]{:S(2)}, u32[]{:S(2)}) collective-permute-start(bf16[768,768]{1,0:T(8,128)(2,1)} %constant_dynamic-update-slice_fusion.8), channel_id=1, source_target_pairs={{0,1},{1,0},{2,3},{3,2},{4,5},{5,4},{6,7},{7,6},{8,9},{9,8},{10,11... | collective-permute-start | bytes 3538952 | tf_op jit(solution)/shard_map/ppermute | solution.py:49
  123.8 12.3 %collective-permute-start.13 = (bf16[2,96,768]{1,2,0:T(8,128)(2,1)}, bf16[2,96,768]{1,2,0:T(8,128)(2,1)}, u32[]{:S(2)}, u32[]{:S(2)}) collective-permute-start(bf16[2,96,768]{1,2,0:T(8,128)(2,1)} %collective-permute-done.11), channel_id=1, source_target_pairs={{0,8},{8,16},{16,24},{24,28},{28,20},{20,12},{12,4},{4,0},{1,9},{9... | collective-permute-start | bytes 884744 | tf_op jit(solution)/shard_map/ppermute | solution.py:62
  127.2 68.6 %collective-permute-start.32 = (bf16[768,768]{1,0:T(8,128)(2,1)}, bf16[768,768]{1,0:T(8,128)(2,1)}, u32[]{:S(2)}, u32[]{:S(2)}) collective-permute-start(bf16[768,768]{1,0:T(8,128)(2,1)} %constant_dynamic-update-slice_fusion.8), channel_id=1, source_target_pairs={{0,2},{1,3},{2,0},{3,1},{4,6},{5,7},{6,4},{7,5},{8,10},{9,11},{10,... | collective-permute-start | bytes 3538952 | tf_op jit(solution)/shard_map/ppermute | solution.py:49
  128.0 13.7 %collective-permute-start.27 = (bf16[2,96,768]{2,1,0:T(8,128)(2,1)}, bf16[2,96,768]{2,1,0:T(8,128)(2,1)}, u32[]{:S(2)}, u32[]{:S(2)}) collective-permute-start(bf16[2,96,768]{2,1,0:T(8,128)(2,1)} %collective-permute-done.25), channel_id=1, source_target_pairs={{0,8},{8,16},{16,24},{24,28},{28,20},{20,12},{12,4},{4,0},{1,9},{9... | collective-permute-start | bytes 884744 | tf_op jit(solution)/shard_map/ppermute | solution.py:62
  129.6 17.1 %collective-permute-start.28 = (bf16[2,96,768]{2,1,0:T(8,128)(2,1)}, bf16[2,96,768]{2,1,0:T(8,128)(2,1)}, u32[]{:S(2)}, u32[]{:S(2)}) collective-permute-start(bf16[2,96,768]{2,1,0:T(8,128)(2,1)} %collective-permute-done.26), channel_id=1, source_target_pairs={{8,0},{16,8},{24,16},{28,24},{20,28},{12,20},{4,12},{0,4},{9,1},{1... | collective-permute-start | bytes 884744 | tf_op jit(solution)/shard_map/ppermute | solution.py:65
  138.0 57.9 %collective-permute-start.14 = (bf16[2,768,768]{2,1,0:T(8,128)(2,1)}, bf16[2,768,768]{2,1,0:T(8,128)(2,1)}, u32[]{:S(2)}, u32[]{:S(2)}) collective-permute-start(bf16[2,768,768]{2,1,0:T(8,128)(2,1)} %constant_dynamic-update-slice_fusion.16), channel_id=1, source_target_pairs={{0,1},{1,0},{2,3},{3,2},{4,5},{5,4},{6,7},{7,6},{8,9},{9,8},{10,11... | collective-permute-start | bytes 7077896 | tf_op jit(solution)/shard_map/ppermute | solution.py:49
  141.7 8.5 %collective-permute-start.29 = (bf16[2,96,768]{2,1,0:T(8,128)(2,1)}, bf16[2,96,768]{2,1,0:T(8,128)(2,1)S(1)}, u32[]{:S(2)}, u32[]{:S(2)}) collective-permute-start(bf16[2,96,768]{2,1,0:T(8,128)(2,1)} %collective-permute-done.27), channel_id=1, source_target_pairs={{0,8},{8,16},{16,24},{24,28},{28,20},{20,12},{12,4},{4,0},{1,9},{9... | collective-permute-start | bytes 884744 | tf_op jit(solution)/shard_map/ppermute | solution.py:62
  151.0 107.0 %collective-permute-start.31 = (bf16[2,768,768]{2,1,0:T(8,128)(2,1)}, bf16[2,768,768]{2,1,0:T(8,128)(2,1)}, u32[]{:S(2)}, u32[]{:S(2)}) collective-permute-start(bf16[2,768,768]{2,1,0:T(8,128)(2,1)} %constant_dynamic-update-slice_fusion), channel_id=1, source_target_pairs={{0,1},{1,0},{2,3},{3,2},{4,5},{5,4},{6,7},{7,6},{8,9},{9,8},{10,11... | collective-permute-start | bytes 7077896 | tf_op jit(solution)/shard_map/ppermute | solution.py:49
  195.8 65.5 %collective-permute-start.33 = (bf16[768,768]{1,0:T(8,128)(2,1)}, bf16[768,768]{1,0:T(8,128)(2,1)}, u32[]{:S(2)}, u32[]{:S(2)}) collective-permute-start(bf16[768,768]{1,0:T(8,128)(2,1)} %collective-permute-done.32), channel_id=1, source_target_pairs={{0,1},{1,0},{2,3},{3,2},{4,5},{5,4},{6,7},{7,6},{8,9},{9,8},{10,11... | collective-permute-start | bytes 3538952 | tf_op jit(solution)/shard_map/ppermute | solution.py:49
  432.7 9.2 %collective-permute-start.65 = (f32[8,384]{1,0:T(8,128)S(1)}, f32[8,384]{1,0:T(8,128)S(1)}, u32[]{:S(2)}, u32[]{:S(2)}) collective-permute-start(f32[8,384]{1,0:T(8,128)S(1)} %get-tuple-element.165), channel_id=1, source_target_pairs={{0,1},{1,0},{2,3},{3,2},{4,5},{5,4},{6,7},{7,6},{8,9},{9,8},{10,11... | collective-permute-start | bytes 36872 | tf_op jit(solution)/shard_map/ppermute | solution.py:49
  432.8 11.3 %collective-permute-start.64 = (f32[8,384]{1,0:T(8,128)S(1)}, f32[8,384]{1,0:T(8,128)S(1)}, u32[]{:S(2)}, u32[]{:S(2)}) collective-permute-start(f32[8,384]{1,0:T(8,128)S(1)} %get-tuple-element.164), channel_id=1, source_target_pairs={{0,1},{1,0},{2,3},{3,2},{4,5},{5,4},{6,7},{7,6},{8,9},{9,8},{10,11... | collective-permute-start | bytes 36872 | tf_op jit(solution)/shard_map/ppermute | solution.py:49
  433.3 26.9 %collective-permute-start.55 = (bf16[768,768]{1,0:T(8,128)(2,1)}, bf16[768,768]{1,0:T(8,128)(2,1)}, u32[]{:S(2)}, u32[]{:S(2)}) collective-permute-start(bf16[768,768]{1,0:T(8,128)(2,1)} %convolution_convert_fusion), channel_id=1, source_target_pairs={{0,1},{1,0},{2,3},{3,2},{4,5},{5,4},{6,7},{7,6},{8,9},{9,8},{10,11... | collective-permute-start | bytes 3538952 | tf_op jit(solution)/shard_map/ppermute | solution.py:49
  433.4 82.4 %collective-permute-start.44 = (bf16[768,768]{1,0:T(8,128)(2,1)}, bf16[768,768]{1,0:T(8,128)(2,1)}, u32[]{:S(2)}, u32[]{:S(2)}) collective-permute-start(bf16[768,768]{1,0:T(8,128)(2,1)} %convolution_convert_fusion.6), channel_id=1, source_target_pairs={{0,1},{1,0},{2,3},{3,2},{4,5},{5,4},{6,7},{7,6},{8,9},{9,8},{10,11... | collective-permute-start | bytes 3538952 | tf_op jit(solution)/shard_map/ppermute | solution.py:49
  433.8 37.1 %collective-permute-start.45 = (bf16[768,768]{1,0:T(8,128)(2,1)}, bf16[768,768]{1,0:T(8,128)(2,1)}, u32[]{:S(2)}, u32[]{:S(2)}) collective-permute-start(bf16[768,768]{1,0:T(8,128)(2,1)} %convolution_convert_fusion.4), channel_id=1, source_target_pairs={{0,1},{1,0},{2,3},{3,2},{4,5},{5,4},{6,7},{7,6},{8,9},{9,8},{10,11... | collective-permute-start | bytes 3538952 | tf_op jit(solution)/shard_map/ppermute | solution.py:49
  449.3 15.2 %collective-permute-start.54 = (bf16[768,768]{1,0:T(8,128)(2,1)}, bf16[768,768]{1,0:T(8,128)(2,1)}, u32[]{:S(2)}, u32[]{:S(2)}) collective-permute-start(bf16[768,768]{1,0:T(8,128)(2,1)} %convolution_convert_fusion.2), channel_id=1, source_target_pairs={{0,1},{1,0},{2,3},{3,2},{4,5},{5,4},{6,7},{7,6},{8,9},{9,8},{10,11... | collective-permute-start | bytes 3538952 | tf_op jit(solution)/shard_map/ppermute | solution.py:49
  454.0 6.2 %collective-permute-start.69 = (f32[1,384]{1,0:T(1,128)S(1)}, f32[1,384]{1,0:T(1,128)S(1)}, u32[]{:S(2)}, u32[]{:S(2)}) collective-permute-start(f32[1,384]{1,0:T(1,128)S(1)} %broadcast_select_fusion.1), channel_id=1, source_target_pairs={{0,4},{4,0},{8,12},{12,8},{16,20},{20,16},{24,28},{28,24},{1,5},{5... | collective-permute-start | bytes 4616 | tf_op jit(solution)/shard_map/ppermute | solution.py:154
  460.2 7.4 %collective-permute-start.35 = (bf16[768,768]{0,1:T(8,128)(2,1)}, bf16[768,768]{0,1:T(8,128)(2,1)S(1)}, u32[]{:S(2)}, u32[]{:S(2)}) collective-permute-start(bf16[768,768]{0,1:T(8,128)(2,1)} %pad_maximum_fusion.1), channel_id=1, source_target_pairs={{0,1},{1,0},{2,3},{3,2},{4,5},{5,4},{6,7},{7,6},{8,9},{9,8},{10,11... | collective-permute-start | bytes 3538952 | tf_op jit(solution)/shard_map/ppermute | solution.py:49
  460.2 9.7 %collective-permute-start.34 = (bf16[768,768]{0,1:T(8,128)(2,1)}, bf16[768,768]{0,1:T(8,128)(2,1)S(1)}, u32[]{:S(2)}, u32[]{:S(2)}) collective-permute-start(bf16[768,768]{0,1:T(8,128)(2,1)} %pad_maximum_fusion), channel_id=1, source_target_pairs={{0,1},{1,0},{2,3},{3,2},{4,5},{5,4},{6,7},{7,6},{8,9},{9,8},{10,11... | collective-permute-start | bytes 3538952 | tf_op jit(solution)/shard_map/ppermute | solution.py:49
  467.3 9.9 %collective-permute-start.56 = (bf16[2,96,768]{2,1,0:T(8,128)(2,1)S(1)}, bf16[2,96,768]{2,1,0:T(8,128)(2,1)S(1)}, u32[]{:S(2)}, u32[]{:S(2)}) collective-permute-start(bf16[2,96,768]{2,1,0:T(8,128)(2,1)S(1)} %get-tuple-element.128), channel_id=1, source_target_pairs={{8,0},{16,8},{24,16},{28,24},{20,28},{12,20},{4,12},{0,4},{9,1},{1... | collective-permute-start | bytes 884744 | tf_op jit(solution)/shard_map/ppermute | solution.py:87
  467.6 17.8 %collective-permute-start.59 = (bf16[2,96,768]{2,1,0:T(8,128)(2,1)S(1)}, bf16[2,96,768]{2,1,0:T(8,128)(2,1)S(1)}, u32[]{:S(2)}, u32[]{:S(2)}) collective-permute-start(bf16[2,96,768]{2,1,0:T(8,128)(2,1)S(1)} %get-tuple-element.129), channel_id=1, source_target_pairs={{0,8},{8,16},{16,24},{24,28},{28,20},{20,12},{12,4},{4,0},{1,9},{9... | collective-permute-start | bytes 884744 | tf_op jit(solution)/shard_map/ppermute | solution.py:80
  470.6 14.2 %collective-permute-start.36 = (bf16[2,96,768]{1,2,0:T(8,128)(2,1)S(1)}, bf16[2,96,768]{1,2,0:T(8,128)(2,1)S(1)}, u32[]{:S(2)}, u32[]{:S(2)}) collective-permute-start(bf16[2,96,768]{1,2,0:T(8,128)(2,1)S(1)} %get-tuple-element.138), channel_id=1, source_target_pairs={{8,0},{16,8},{24,16},{28,24},{20,28},{12,20},{4,12},{0,4},{9,1},{1... | collective-permute-start | bytes 884744 | tf_op jit(solution)/shard_map/ppermute | solution.py:87
  475.8 41.5 %collective-permute-start.46 = (bf16[768,768]{1,0:T(8,128)(2,1)}, bf16[768,768]{1,0:T(8,128)(2,1)}, u32[]{:S(2)}, u32[]{:S(2)}) collective-permute-start(bf16[768,768]{1,0:T(8,128)(2,1)} %add_convert_fusion.4), channel_id=1, source_target_pairs={{0,2},{1,3},{2,0},{3,1},{4,6},{5,7},{6,4},{7,5},{8,10},{9,11},{10,... | collective-permute-start | bytes 3538952 | tf_op jit(solution)/shard_map/ppermute | solution.py:49
  477.2 20.2 %collective-permute-start.39 = (bf16[2,96,768]{1,2,0:T(8,128)(2,1)S(1)}, bf16[2,96,768]{1,2,0:T(8,128)(2,1)S(1)}, u32[]{:S(2)}, u32[]{:S(2)}) collective-permute-start(bf16[2,96,768]{1,2,0:T(8,128)(2,1)S(1)} %get-tuple-element.139), channel_id=1, source_target_pairs={{0,8},{8,16},{16,24},{24,28},{28,20},{20,12},{12,4},{4,0},{1,9},{9... | collective-permute-start | bytes 884744 | tf_op jit(solution)/shard_map/ppermute | solution.py:80
  484.8 9.9 %collective-permute-start.57 = (bf16[2,96,768]{2,1,0:T(8,128)(2,1)S(1)}, bf16[2,96,768]{2,1,0:T(8,128)(2,1)S(1)}, u32[]{:S(2)}, u32[]{:S(2)}) collective-permute-start(bf16[2,96,768]{2,1,0:T(8,128)(2,1)S(1)} %add_convert_fusion.20), channel_id=1, source_target_pairs={{8,0},{16,8},{24,16},{28,24},{20,28},{12,20},{4,12},{0,4},{9,1},{1... | collective-permute-start | bytes 884744 | tf_op jit(solution)/shard_map/ppermute | solution.py:87
  485.3 16.2 %collective-permute-start.37 = (bf16[2,96,768]{1,2,0:T(8,128)(2,1)S(1)}, bf16[2,96,768]{1,2,0:T(8,128)(2,1)S(1)}, u32[]{:S(2)}, u32[]{:S(2)}) collective-permute-start(bf16[2,96,768]{1,2,0:T(8,128)(2,1)S(1)} %add_convert_fusion.15), channel_id=1, source_target_pairs={{8,0},{16,8},{24,16},{28,24},{20,28},{12,20},{4,12},{0,4},{9,1},{1... | collective-permute-start | bytes 884744 | tf_op jit(solution)/shard_map/ppermute | solution.py:87
  495.7 11.3 %collective-permute-start.60 = (bf16[2,96,768]{2,1,0:T(8,128)(2,1)}, bf16[2,96,768]{2,1,0:T(8,128)(2,1)}, u32[]{:S(2)}, u32[]{:S(2)}) collective-permute-start(bf16[2,96,768]{2,1,0:T(8,128)(2,1)} %get-tuple-element.127), channel_id=1, source_target_pairs={{0,8},{8,16},{16,24},{24,28},{28,20},{20,12},{12,4},{4,0},{1,9},{9... | collective-permute-start | bytes 884744 | tf_op jit(solution)/shard_map/ppermute | solution.py:80
  502.9 9.9 %collective-permute-start.40 = (bf16[2,96,768]{1,2,0:T(8,128)(2,1)}, bf16[2,96,768]{1,2,0:T(8,128)(2,1)}, u32[]{:S(2)}, u32[]{:S(2)}) collective-permute-start(bf16[2,96,768]{1,2,0:T(8,128)(2,1)} %get-tuple-element.137), channel_id=1, source_target_pairs={{0,8},{8,16},{16,24},{24,28},{28,20},{20,12},{12,4},{4,0},{1,9},{9... | collective-permute-start | bytes 884744 | tf_op jit(solution)/shard_map/ppermute | solution.py:80
  506.7 38.6 %collective-permute-start.58 = (bf16[2,96,768]{2,1,0:T(8,128)(2,1)}, bf16[2,96,768]{2,1,0:T(8,128)(2,1)S(1)}, u32[]{:S(2)}, u32[]{:S(2)}) collective-permute-start(bf16[2,96,768]{2,1,0:T(8,128)(2,1)} %get-tuple-element.126), channel_id=1, source_target_pairs={{8,0},{16,8},{24,16},{28,24},{20,28},{12,20},{4,12},{0,4},{9,1},{1... | collective-permute-start | bytes 884744 | tf_op jit(solution)/shard_map/ppermute | solution.py:87
  507.0 40.7 %collective-permute-start.38 = (bf16[2,96,768]{1,2,0:T(8,128)(2,1)}, bf16[2,96,768]{1,2,0:T(8,128)(2,1)S(1)}, u32[]{:S(2)}, u32[]{:S(2)}) collective-permute-start(bf16[2,96,768]{1,2,0:T(8,128)(2,1)} %get-tuple-element.136), channel_id=1, source_target_pairs={{8,0},{16,8},{24,16},{28,24},{20,28},{12,20},{4,12},{0,4},{9,1},{1... | collective-permute-start | bytes 884744 | tf_op jit(solution)/shard_map/ppermute | solution.py:87
  512.8 10.0 %collective-permute-start.61 = (bf16[2,96,768]{2,1,0:T(8,128)(2,1)S(1)}, bf16[2,96,768]{2,1,0:T(8,128)(2,1)S(1)}, u32[]{:S(2)}, u32[]{:S(2)}) collective-permute-start(bf16[2,96,768]{2,1,0:T(8,128)(2,1)S(1)} %add_convert_fusion.17), channel_id=1, source_target_pairs={{0,8},{8,16},{16,24},{24,28},{28,20},{20,12},{12,4},{4,0},{1,9},{9... | collective-permute-start | bytes 884744 | tf_op jit(solution)/shard_map/ppermute | solution.py:80
  515.7 17.6 %collective-permute-start.41 = (bf16[2,96,768]{1,2,0:T(8,128)(2,1)S(1)}, bf16[2,96,768]{1,2,0:T(8,128)(2,1)S(1)}, u32[]{:S(2)}, u32[]{:S(2)}) collective-permute-start(bf16[2,96,768]{1,2,0:T(8,128)(2,1)S(1)} %add_convert_fusion.12), channel_id=1, source_target_pairs={{0,8},{8,16},{16,24},{24,28},{28,20},{20,12},{12,4},{4,0},{1,9},{9... | collective-permute-start | bytes 884744 | tf_op jit(solution)/shard_map/ppermute | solution.py:80
  519.4 12.2 %collective-permute-start.50 = (bf16[96,768]{1,0:T(8,128)(2,1)S(1)}, bf16[96,768]{1,0:T(8,128)(2,1)S(1)}, u32[]{:S(2)}, u32[]{:S(2)}) collective-permute-start(bf16[96,768]{1,0:T(8,128)(2,1)S(1)} %get-tuple-element.135), channel_id=1, source_target_pairs={{0,8},{8,16},{16,24},{24,28},{28,20},{20,12},{12,4},{4,0},{1,9},{9... | collective-permute-start | bytes 442376 | tf_op jit(solution)/shard_map/ppermute | solution.py:80
  522.8 12.4 %collective-permute-start.47 = (bf16[96,768]{1,0:T(8,128)(2,1)S(1)}, bf16[96,768]{1,0:T(8,128)(2,1)S(1)}, u32[]{:S(2)}, u32[]{:S(2)}) collective-permute-start(bf16[96,768]{1,0:T(8,128)(2,1)S(1)} %get-tuple-element.134), channel_id=1, source_target_pairs={{8,0},{16,8},{24,16},{28,24},{20,28},{12,20},{4,12},{0,4},{9,1},{1... | collective-permute-start | bytes 442376 | tf_op jit(solution)/shard_map/ppermute | solution.py:87
  531.6 15.3 %collective-permute-start.62 = (bf16[2,96,768]{2,1,0:T(8,128)(2,1)S(1)}, bf16[2,96,768]{2,1,0:T(8,128)(2,1)S(1)}, u32[]{:S(2)}, u32[]{:S(2)}) collective-permute-start(bf16[2,96,768]{2,1,0:T(8,128)(2,1)S(1)} %add_convert_fusion.16), channel_id=1, source_target_pairs={{0,8},{8,16},{16,24},{24,28},{28,20},{20,12},{12,4},{4,0},{1,9},{9... | collective-permute-start | bytes 884744 | tf_op jit(solution)/shard_map/ppermute | solution.py:80
  533.3 11.4 %collective-permute-start.51 = (bf16[96,768]{1,0:T(8,128)(2,1)S(1)}, bf16[96,768]{1,0:T(8,128)(2,1)S(1)}, u32[]{:S(2)}, u32[]{:S(2)}) collective-permute-start(bf16[96,768]{1,0:T(8,128)(2,1)S(1)} %add_convert_fusion.23), channel_id=1, source_target_pairs={{0,8},{8,16},{16,24},{24,28},{28,20},{20,12},{12,4},{4,0},{1,9},{9... | collective-permute-start | bytes 442376 | tf_op jit(solution)/shard_map/ppermute | solution.py:80
  535.1 15.3 %collective-permute-start.42 = (bf16[2,96,768]{1,2,0:T(8,128)(2,1)S(1)}, bf16[2,96,768]{1,2,0:T(8,128)(2,1)S(1)}, u32[]{:S(2)}, u32[]{:S(2)}) collective-permute-start(bf16[2,96,768]{1,2,0:T(8,128)(2,1)S(1)} %add_convert_fusion.11), channel_id=1, source_target_pairs={{0,8},{8,16},{16,24},{24,28},{28,20},{20,12},{12,4},{4,0},{1,9},{9... | collective-permute-start | bytes 884744 | tf_op jit(solution)/shard_map/ppermute | solution.py:80
  544.8 6.7 %collective-permute-start.48 = (bf16[96,768]{1,0:T(8,128)(2,1)S(1)}, bf16[96,768]{1,0:T(8,128)(2,1)S(1)}, u32[]{:S(2)}, u32[]{:S(2)}) collective-permute-start(bf16[96,768]{1,0:T(8,128)(2,1)S(1)} %get-tuple-element.132), channel_id=1, source_target_pairs={{8,0},{16,8},{24,16},{28,24},{20,28},{12,20},{4,12},{0,4},{9,1},{1... | collective-permute-start | bytes 442376 | tf_op jit(solution)/shard_map/ppermute | solution.py:87
  545.3 7.7 %collective-permute-start.52 = (bf16[96,768]{1,0:T(8,128)(2,1)S(1)}, bf16[96,768]{1,0:T(8,128)(2,1)S(1)}, u32[]{:S(2)}, u32[]{:S(2)}) collective-permute-start(bf16[96,768]{1,0:T(8,128)(2,1)S(1)} %get-tuple-element.133), channel_id=1, source_target_pairs={{0,8},{8,16},{16,24},{24,28},{28,20},{20,12},{12,4},{4,0},{1,9},{9... | collective-permute-start | bytes 442376 | tf_op jit(solution)/shard_map/ppermute | solution.py:80
  547.0 12.4 %collective-permute-start.63 = (bf16[96,768]{1,0:T(8,128)(2,1)S(1)}, bf16[96,768]{1,0:T(8,128)(2,1)S(1)}, u32[]{:S(2)}, u32[]{:S(2)}) collective-permute-start(bf16[96,768]{1,0:T(8,128)(2,1)S(1)} %fusion.78), channel_id=1, source_target_pairs={{0,2},{1,3},{2,0},{3,1},{4,6},{5,7},{6,4},{7,5},{8,10},{9,11},{10,... | collective-permute-start | bytes 442376 | tf_op jit(solution)/shard_map/ppermute | solution.py:49
  550.7 5.7 %collective-permute-start.43 = (bf16[96,768]{0,1:T(8,128)(2,1)S(1)}, bf16[96,768]{0,1:T(8,128)(2,1)S(1)}, u32[]{:S(2)}, u32[]{:S(2)}) collective-permute-start(bf16[96,768]{0,1:T(8,128)(2,1)S(1)} %fusion.77), channel_id=1, source_target_pairs={{0,2},{1,3},{2,0},{3,1},{4,6},{5,7},{6,4},{7,5},{8,10},{9,11},{10,... | collective-permute-start | bytes 442376 | tf_op jit(solution)/shard_map/ppermute | solution.py:49
  553.0 7.1 %collective-permute-start.49 = (bf16[96,768]{1,0:T(8,128)(2,1)S(1)}, bf16[96,768]{1,0:T(8,128)(2,1)S(1)}, u32[]{:S(2)}, u32[]{:S(2)}) collective-permute-start(bf16[96,768]{1,0:T(8,128)(2,1)S(1)} %get-tuple-element.130), channel_id=1, source_target_pairs={{8,0},{16,8},{24,16},{28,24},{20,28},{12,20},{4,12},{0,4},{9,1},{1... | collective-permute-start | bytes 442376 | tf_op jit(solution)/shard_map/ppermute | solution.py:87
  553.1 7.0 %collective-permute-start.53 = (bf16[96,768]{1,0:T(8,128)(2,1)S(1)}, bf16[96,768]{1,0:T(8,128)(2,1)S(1)}, u32[]{:S(2)}, u32[]{:S(2)}) collective-permute-start(bf16[96,768]{1,0:T(8,128)(2,1)S(1)} %get-tuple-element.131), channel_id=1, source_target_pairs={{0,8},{8,16},{16,24},{24,28},{28,20},{20,12},{12,4},{4,0},{1,9},{9... | collective-permute-start | bytes 442376 | tf_op jit(solution)/shard_map/ppermute | solution.py:80
  (89 other events, 799.1 us)
